TPU v7x, 32 devices: a whole 2x2x4 slice. The times are simulated.
32 devices in a mesh: gx: 4 (over y, core), gy: 8 (over z, x).
Axes of the slice: x: 2, y: 2, z: 4, core: 2. Of those that a mesh axis runs over, the one named last changes fastest.
Arguments:
- displacement: float32 [3, 32, 64, 128], P(None, 'gx', 'gy'), may hold values from -0.12 to 0.12
- velocity: float32 [3, 32, 64, 128], P(None, 'gx', 'gy'), may hold values from -4 to 4
- intact: int32 [61, 32, 64, 128], P(None, 'gx', 'gy'), may hold values 0 or 1
- material: int32 [32, 64, 128], P('gx', 'gy'), may hold values from 0 to 7
- bulk_modulus: float32 [8], replicated, may hold values from 80 to 800
- shear_modulus: float32 [8], replicated, may hold values from 40 to 400
- density: float32 [8], replicated, may hold values from 1 to 4
Outputs:
- new_displacement: float32 [3, 32, 64, 128], P(None, 'gx', 'gy')
- new_velocity: float32 [3, 32, 64, 128], P(None, 'gx', 'gy')
- last_force: float32 [3, 32, 64, 128], P(None, 'gx', 'gy')
Inputs may be any that keep to these rules, and one draw needn't show every extreme that they name: intact[k, i] refers to the bond from node i to node i + e_k.
All inputs are finite; a program needn't handle non-finite values. No bound on the sum of `intact` on one device may be relied on, other than what follows from the above.
Results may differ from a plain program's by a relative error of at most 0.00002.
Values sent between devices are 32-bit elements; how exact they have to be, the bound alone decides.
A program may use at most 64 MiB of HBM per device.

v0:
```python
import functools
import math

import jax
import jax.numpy as jnp
from jax import lax
from jax.experimental import pallas as pl
from jax.experimental.pallas import tpu as pltpu
from jax.sharding import PartitionSpec as P

STEPS = 2
TIME_STEP = 0.02
REACH = 3
NEAR = 2
MESH = pl.DeviceIdType.MESH
F32 = jnp.float32

AROUND = [(dx, dy) for dx in (-1, 0, 1) for dy in (-1, 0, 1) if (dx, dy) != (0, 0)]
STATE = [("S", (-1, 0)), ("S", (0, -1)), ("S", (0, 1)), ("S", (-1, -1)), ("S", (-1, 1))]
CHUNKS = {
    "C": [("C", (1, 0)), ("C", (1, -1)), ("C", (1, 1)), ("C", (0, -1)), ("C", (0, 1))],
    "A": [("A", (-1, 0)), ("A", (-1, -1)), ("A", (-1, 1)), ("A", (0, -1)), ("A", (0, 1))],
    "B": [("B", (0, -1)), ("B", (0, 1))],
}
FINAL = {
    "C": [("C", (1, 0)), ("C", (1, -1)), ("C", (1, 1))],
    "A": [("A", (0, -1)), ("A", (0, 1))],
    "B": [("B", (0, -1)), ("B", (0, 1))],
}
SLOT = {key: n for n, key in enumerate(CHUNKS["C"] + CHUNKS["A"] + CHUNKS["B"])}
SLOT.update({key: n for n, key in enumerate(STATE)})


def half_offsets():
    span = range(-REACH, REACH + 1)
    return [
        (a, b, c)
        for a in span
        for b in span
        for c in span
        if a * a + b * b + c * c <= REACH * REACH and (a, b, c) > (0, 0, 0)
    ]


OFFSETS = half_offsets()
GROUPS = {}
for _k, (_a, _b, _c) in enumerate(OFFSETS):
    GROUPS.setdefault((_a, _b), []).append((_k, _c))
RADII = [math.sqrt(float(a * a + b * b + c * c)) for a, b, c in OFFSETS]
VOLUME = 2.0 * sum(RADII)


def round_up(value, unit):
    return -(-value // unit) * unit


def tree_sum(terms):
    while len(terms) > 1:
        terms = [
            terms[n] + terms[n + 1] if n + 1 < len(terms) else terms[n]
            for n in range(0, len(terms), 2)
        ]
    return terms[0]


def kernel(
    grid_rows,
    grid_cols,
    u_hbm,
    v_hbm,
    intact_hbm,
    mat_hbm,
    bulk_hbm,
    shear_hbm,
    dens_hbm,
    out_u,
    out_v,
    out_f,
    u_ref,
    mat_ref,
    bulk_ref,
    shear_ref,
    dens_ref,
    intact_ref,
    flag,
    by_inverse,
    by_stretch,
    wide_u,
    wide_v,
    u_shift,
    a_shift,
    b_shift,
    a_coef,
    inertia,
    strain,
    force,
    vm,
    pack_u,
    pack_vm,
    pack_t,
    pack_f,
    u_x,
    u_y,
    u_d,
    vm_x,
    vm_y,
    vm_d,
    t_x,
    t_y,
    t_d,
    f_x,
    f_y,
    f_d,
    local_sem,
    send_sem,
    recv_sem,
):
    rows, cols, nz = mat_ref.shape
    wide_rows = rows + REACH
    padded = wide_u.shape[2]
    gx = lax.axis_index("gx")
    gy = lax.axis_index("gy")

    def present(direction):
        x = gx + direction[0]
        y = gy + direction[1]
        return (x >= 0) & (x < grid_rows) & (y >= 0) & (y < grid_cols)

    here = {direction: present(direction) for direction in AROUND}

    barrier = pltpu.get_barrier_semaphore()
    for direction in AROUND:

        @pl.when(here[direction])
        def _(direction=direction):
            pl.semaphore_signal(
                barrier,
                inc=1,
                device_id=(gx + direction[0], gy + direction[1]),
                device_id_type=MESH,
            )

    loads = [
        pltpu.make_async_copy(source, target, local_sem.at[n])
        for n, (source, target) in enumerate(
            [
                (u_hbm, u_ref),
                (v_hbm, vm.at[0:3]),
                (mat_hbm, mat_ref),
                (intact_hbm, intact_ref),
                (bulk_hbm, bulk_ref),
                (shear_hbm, shear_ref),
                (dens_hbm, dens_ref),
            ]
        )
    ]
    for load in loads:
        load.start()

    loads[0].wait()
    for comp in range(3):
        for r in range(rows):
            pack_u[0, comp, 3 * r : 3 * r + 3] = u_ref[comp, r, 0:3]
            pack_u[1, comp, 3 * r : 3 * r + 3] = u_ref[comp, r, cols - 3 : cols]

    on_x = (gx > 0).astype(jnp.int32) + (gx < grid_rows - 1).astype(jnp.int32)
    on_y = (gy > 0).astype(jnp.int32) + (gy < grid_cols - 1).astype(jnp.int32)
    pl.semaphore_wait(barrier, (1 + on_x) * (1 + on_y) - 1)

    def copy_to(stage, key, source, target):
        dx, dy = key[1]
        return pltpu.make_async_remote_copy(
            src_ref=source,
            dst_ref=target,
            send_sem=send_sem.at[stage, SLOT[key]],
            recv_sem=recv_sem.at[stage, SLOT[key]],
            device_id=(gx + dx, gy + dy),
            device_id_type=MESH,
        )

    def side(value):
        return 0 if value < 0 else 1

    def state_source(key, whole, pack):
        dx, dy = key[1]
        if dy == 0:
            return whole.at[:, 0:REACH]
        if dx == 0:
            return pack.at[side(dy)]
        return pack.at[side(dy), :, 0:16]

    def state_target(key, x_buf, y_buf, d_buf):
        dx, dy = key[1]
        if dy == 0:
            return x_buf
        if dx == 0:
            return y_buf.at[side(-dy)]
        return d_buf.at[side(-dy)]

    rows_of = {"A": (0, REACH), "B": (REACH, rows), "C": (rows, wide_rows)}
    wide_a = round_up(6 * REACH, 8)
    wide_b = round_up(6 * (rows - REACH), 8)
    start_of = {"A": 0, "B": wide_a, "C": wide_a + wide_b}

    def packed_rows(chunk, final):
        first, end = rows_of[chunk]
        start = start_of[chunk]
        return slice(start, start + round_up((3 if final else 6) * (end - first), 8))

    def sum_source(key, whole, pack, final):
        chunk, (dx, dy) = key
        if dy == 0:
            return whole.at[:, slice(*rows_of[chunk])]
        return pack.at[side(dy), :, packed_rows(chunk, final)]

    def sum_target(key, x_buf, y_buf, d_buf, step, final):
        chunk, (dx, dy) = key
        if dy == 0:
            return x_buf.at[step, side(-dx)]
        span = packed_rows(chunk, final)
        if dx == 0:
            return y_buf.at[step, side(-dy), :, span]
        return d_buf.at[step, 2 * side(-dx) + side(-dy), :, 0 : span.stop - span.start]

    def start_all(stage, keys, source_of, target_of):
        for key in keys:

            @pl.when(here[key[1]])
            def _(key=key):
                copy_to(stage, key, source_of(key), target_of(key)).start()

    def wait_recv(stage, key, source_of, target_of):
        target = target_of(key)
        pltpu.make_async_remote_copy(
            src_ref=target,
            dst_ref=target,
            send_sem=send_sem.at[stage, SLOT[key]],
            recv_sem=recv_sem.at[stage, SLOT[key]],
            device_id=(gx - key[1][0], gy - key[1][1]),
            device_id_type=MESH,
        ).wait_recv()

    def wait_sends(stage, keys, source_of, target_of):
        for key in keys:

            @pl.when(here[key[1]])
            def _(key=key):
                copy_to(stage, key, source_of(key), target_of(key)).wait_send()

    u_plan = (
        lambda d: state_source(d, u_ref, pack_u),
        lambda o: state_target(o, u_x, u_y, u_d),
    )
    vm_plan = (
        lambda d: state_source(d, vm, pack_vm),
        lambda o: state_target(o, vm_x, vm_y, vm_d),
    )
    start_all(0, STATE, *u_plan)
    loads[1].wait()
    loads[2].wait()
    vm[3] = mat_ref[...].astype(F32)
    for comp in range(4):
        for r in range(rows):
            pack_vm[0, comp, 3 * r : 3 * r + 3] = vm[comp, r, 0:3]
            pack_vm[1, comp, 3 * r : 3 * r + 3] = vm[comp, r, cols - 3 : cols]
    start_all(1, STATE, *vm_plan)

    def shifted(values, c):
        if c == 0:
            return values
        lane = lax.broadcasted_iota(jnp.int32, values.shape, 1)
        moved = pltpu.roll(values, (-c) % nz, axis=1)
        return jnp.where((lane + c >= 0) & (lane + c < nz), moved, 0.0)

    def take_state(stage, plan, wide_of, comps):
        for key in STATE:
            origin = (-key[1][0], -key[1][1])

            @pl.when(here[origin])
            def _(key=key, origin=origin):
                wait_recv(stage, key, *plan)
                dx, dy = origin
                buf = plan[1](key)
                for comp in range(comps):
                    wide = wide_of(comp)
                    if dy == 0:
                        for r in range(REACH):
                            wide[rows + r, REACH : REACH + cols] = buf[comp, r]
                        continue
                    at = 0 if dy < 0 else REACH + cols
                    for r in range(rows if dx == 0 else REACH):
                        row = r if dx == 0 else rows + r
                        wide[row, at : at + REACH] = buf[comp, 3 * r : 3 * r + 3]


    wide_u[...] = jnp.zeros(wide_u.shape, F32)
    wide_v[...] = jnp.zeros(wide_v.shape, F32)
    for comp in range(3):
        wide_u[comp, 0:rows, REACH : REACH + cols] = u_ref[comp]
    for comp in range(4):
        wide_v[comp, 0:rows, REACH : REACH + cols] = vm[comp]

    def shift_motion():
        @pl.loop(0, wide_rows)
        def _(r):
            for comp in range(3):
                values = wide_u[comp, r]
                for c in range(-NEAR, NEAR + 1):
                    moved = shifted(values, c)
                    if comp == 2 and c != 0:
                        moved = moved + float(c)
                    u_shift[c + NEAR, comp, r] = moved

    def materials():
        @pl.loop(0, wide_rows)
        def _(r):
            classes = wide_v[3, r]
            bulk = jnp.full(classes.shape, bulk_ref[0], F32)
            shear = jnp.full(classes.shape, shear_ref[0], F32)
            dens = jnp.full(classes.shape, dens_ref[0], F32)
            for number in range(1, bulk_ref.shape[0]):
                match = classes == float(number)
                bulk = jnp.where(match, bulk_ref[number], bulk)
                shear = jnp.where(match, shear_ref[number], shear)
                dens = jnp.where(match, dens_ref[number], dens)
            inertia[r] = TIME_STEP / dens
            a_coef[r] = (9.0 / (VOLUME * VOLUME)) * (bulk - (5.0 / 3.0) * shear)
            stiff = (15.0 / VOLUME) * shear
            for c in range(-NEAR, NEAR + 1):
                b_shift[c + NEAR, r] = shifted(stiff, c)

    depth = lax.broadcasted_iota(jnp.int32, (cols, nz), 1)
    column = lax.broadcasted_iota(jnp.int32, (cols, nz), 0) + gy * cols

    def partner(buffer, i, a, b, c, own):
        if c > NEAR:
            return shifted(own, c)
        return buffer[c + NEAR, i + a, pl.ds(REACH + b, cols)]

    def bond_vector(i, a, b, c, own):
        y = []
        for comp in range(3):
            if c > NEAR:
                there = shifted(own[3][comp], c)
                if comp == 2:
                    there = there + float(c)
            else:
                there = u_shift[c + NEAR, comp, i + a, pl.ds(REACH + b, cols)]
            y.append(there - (own[0][a], own[1][b], own[2])[comp])
        return y

    def geometry(i, a, b, c, own):
        y0, y1, y2 = bond_vector(i, a, b, c, own)
        square = y0 * y0 + y1 * y1 + y2 * y2
        inverse = lax.rsqrt(square)
        return square * inverse, inverse

    def own_motion(i):
        mine = [wide_u[comp, i, REACH : REACH + cols] for comp in range(3)]
        by_row = {a: mine[0] - float(a) for a in range(REACH + 1)}
        by_col = {b: mine[1] - float(b) for b in range(-REACH, REACH + 1)}
        return (by_row, by_col, mine[2], mine)

    def back(values, c):
        return values if c == 0 else pltpu.roll(values, c % nz, axis=1)

    def order(t):
        return lax.rem(t + rows - REACH, rows)

    def send_done(t, stage, keys, plan, whole, pack, final):
        @pl.when(t == REACH - 1)
        def _():
            pack_sums(whole, pack, "C", final)
            start_all(stage, keys["C"], *plan)

        @pl.when(t == 2 * REACH - 1)
        def _():
            pack_sums(whole, pack, "A", final)
            start_all(stage, keys["A"], *plan)

    def weights():
        @pl.loop(0, rows)
        def _(i):
            lane_in = {
                c: jnp.where((depth + c >= 0) & (depth + c < nz), 1.0, 0.0)
                for c in range(-NEAR, REACH + 1)
            }
            for (a, b), members in GROUPS.items():
                row_in = (gx * rows + i + a) < grid_rows * rows
                plane = jnp.where(
                    (column + b >= 0) & (column + b < grid_cols * cols) & row_in, 1.0, 0.0
                )
                for k, c in members:
                    flag[k, i] = intact_ref[k, i].astype(F32) * (plane * lane_in[c])

    def prepare():
        @pl.loop(0, rows)
        def _(i):
            own_b = b_shift[NEAR, i, pl.ds(REACH, cols)]
            for k, (a, b, c) in enumerate(OFFSETS):
                both_b = own_b + partner(b_shift, i, a, b, c, own_b)
                scale = flag[k, i] * by_inverse[k, i]
                by_stretch[k, i] = scale * (both_b * (by_stretch[k, i] * (1.0 / RADII[k])))
                by_inverse[k, i] = scale

    def strain_pass(send):
        strain[...] = jnp.zeros(strain.shape, F32)

        @pl.loop(0, rows)
        def _(t):
            i = order(t)
            own = own_motion(i)
            sums = []
            for (a, b), members in GROUPS.items():
                returned = []
                for k, c in members:
                    length, inverse = geometry(i, a, b, c, own)
                    stretch = length - RADII[k]
                    by_inverse[k, i] = inverse
                    by_stretch[k, i] = stretch
                    term = flag[k, i] * stretch
                    sums.append(term)
                    returned.append(back(term, c))
                at = pl.ds(REACH + b, cols)
                strain[0, i + a, at] = strain[0, i + a, at] + tree_sum(returned)
                sums = [tree_sum(sums)]
            at = pl.ds(REACH, cols)
            strain[0, i, at] = strain[0, i, at] + sums[0]
            send(t)

    def force_pass(send):
        force[...] = jnp.zeros(force.shape, F32)

        @pl.loop(0, rows)
        def _(t):
            i = order(t)
            own = own_motion(i)
            mid = pl.ds(REACH, cols)
            own_a = a_shift[NEAR, i, mid]
            sums = [[], [], []]
            for (a, b), members in GROUPS.items():
                at = pl.ds(REACH + b, cols)
                returned = [[], [], []]
                for k, c in members:
                    y = bond_vector(i, a, b, c, own)
                    both_a = own_a + partner(a_shift, i, a, b, c, own_a)
                    tension = by_inverse[k, i] * both_a + by_stretch[k, i]
                    for comp in range(3):
                        term = tension * y[comp]
                        sums[comp].append(term)
                        returned[comp].append(back(term, c))
                for comp in range(3):
                    force[comp, i + a, at] = force[comp, i + a, at] - tree_sum(returned[comp])
                    sums[comp] = [tree_sum(sums[comp])]
            for comp in range(3):
                force[comp, i, mid] = force[comp, i, mid] + sums[comp][0]

            send(t)

    def pack_sums(whole, pack, chunk, final):
        first, end = rows_of[chunk]
        start = start_of[chunk]
        width = 3 if final else 6
        high = cols + REACH if final else cols
        for comp in range(whole.shape[0]):
            for n, r in enumerate(range(first, end)):
                at = start + width * n
                pack[0, comp, at : at + width] = whole[comp, r, 0:width]
                pack[1, comp, at : at + width] = whole[comp, r, high : high + width]

    def take_sums(stage, keys, plan, whole, comps, final):
        wait_sends(stage, [key for key in keys["C"] + keys["A"] if key[1][1] == 0], *plan)
        width = 3 if final else 6
        for key in keys["C"] + keys["A"] + keys["B"]:
            chunk, direction = key
            origin = (-direction[0], -direction[1])

            @pl.when(here[origin])
            def _(key=key, chunk=chunk, origin=origin):
                wait_recv(stage, key, *plan)
                dx, dy = origin
                buf = plan[1](key)
                first, end = rows_of[chunk]
                first = first + dx * rows
                for comp in range(comps):
                    for n in range(end - rows_of[chunk][0]):
                        if dy == 0:
                            whole[comp, first + n] = whole[comp, first + n] + buf[comp, n]
                            continue
                        low = REACH if final else 0
                        at = pl.ds(low if dy < 0 else cols, width)
                        whole[comp, first + n, at] = (
                            whole[comp, first + n, at] + buf[comp, width * n : width * n + width]
                        )

    def finish_sends(stage, keys, plan):
        rest = keys["C"] + keys["A"] + keys["B"]
        wait_sends(stage, [key for key in rest if key[1][1] != 0], *plan)

    for load in loads[3:]:
        load.wait()
    weights()
    take_state(0, u_plan, lambda comp: wide_u.at[comp], 3)
    shift_motion()

    for step in range(STEPS):
        last = step == STEPS - 1
        stage = 2 + 2 * step
        t_plan = (
            lambda key: sum_source(key, strain, pack_t, False),
            lambda key, step=step: sum_target(key, t_x, t_y, t_d, step, False),
        )
        strain_pass(
            lambda t, stage=stage, t_plan=t_plan: send_done(
                t, stage, CHUNKS, t_plan, strain, pack_t, False
            ),
        )
        pack_sums(strain, pack_t, "B", False)
        start_all(stage, CHUNKS["B"], *t_plan)
        if step == 0:
            take_state(1, vm_plan, lambda comp: wide_v.at[comp], 4)
            materials()
        prepare()
        take_sums(stage, CHUNKS, t_plan, strain, 1, False)

        @pl.loop(0, wide_rows)
        def _(r):
            values = strain[0, r] * a_coef[r]
            for c in range(-NEAR, NEAR + 1):
                a_shift[c + NEAR, r] = shifted(values, c)

        finish_sends(stage, CHUNKS, t_plan)
        stage = stage + 1
        keys = FINAL if last else CHUNKS
        f_plan = (
            lambda key, last=last: sum_source(key, force, pack_f, last),
            lambda key, step=step, last=last: sum_target(key, f_x, f_y, f_d, step, last),
        )
        force_pass(
            lambda t, stage=stage, keys=keys, f_plan=f_plan, last=last: send_done(
                t, stage, keys, f_plan, force, pack_f, last
            )
        )
        pack_sums(force, pack_f, "B", last)
        start_all(stage, keys["B"], *f_plan)
        take_sums(stage, keys, f_plan, force, 3, last)
        if not last:

            @pl.loop(0, wide_rows)
            def _(r):
                for comp in range(3):
                    speed = wide_v[comp, r] + force[comp, r] * inertia[r]
                    wide_v[comp, r] = speed
                    wide_u[comp, r] = wide_u[comp, r] + TIME_STEP * speed

            shift_motion()
            finish_sends(stage, keys, f_plan)
        else:
            mid = pl.ds(REACH, cols)

            @pl.loop(0, rows)
            def _(r):
                for comp in range(3):
                    pull = force[comp, r, mid]
                    speed = wide_v[comp, r, mid] + pull * inertia[r, mid]
                    out_f[comp, r] = pull
                    out_v[comp, r] = speed
                    out_u[comp, r] = wide_u[comp, r, mid] + TIME_STEP * speed

            finish_sends(stage, keys, f_plan)
            wait_sends(0, STATE, *u_plan)
            wait_sends(1, STATE, *vm_plan)


def hand_over(u_in, v_in, f_in, u_out, v_out, f_out):
    u_out[...] = u_in[...]
    v_out[...] = v_in[...]
    f_out[...] = f_in[...]


def on_device(displacement, velocity, intact, material, bulk_modulus, shear_modulus, density):
    rows, cols, nz = material.shape
    wide_rows = rows + REACH
    padded = round_up(cols + 2 * REACH, 8)
    packed = 2 * round_up(6 * REACH, 8) + round_up(6 * (rows - REACH), 8)
    own = jax.ShapeDtypeStruct((3, rows, cols, nz), F32)
    vmem = pl.BlockSpec(memory_space=pltpu.VMEM)
    hbm = pl.BlockSpec(memory_space=pltpu.HBM)
    table = pltpu.SMEM(bulk_modulus.shape, F32)
    stages = 2 + 2 * STEPS

    def buffer(*shape):
        return pltpu.VMEM(shape + (nz,), F32)

    results = pl.pallas_call(
        functools.partial(kernel, lax.axis_size("gx"), lax.axis_size("gy")),
        out_shape=(own, own, own),
        in_specs=[hbm] * 7,
        out_specs=(vmem, vmem, vmem),
        scratch_shapes=[
            buffer(3, rows, cols),
            pltpu.VMEM(material.shape, jnp.int32),
            table,
            table,
            table,
            pltpu.VMEM(intact.shape, jnp.int32),
            pltpu.VMEM(intact.shape, F32),
            pltpu.VMEM(intact.shape, F32),
            pltpu.VMEM(intact.shape, F32),
            buffer(3, wide_rows, padded),
            buffer(4, wide_rows, padded),
            buffer(5, 3, wide_rows, padded),
            buffer(5, wide_rows, padded),
            buffer(5, wide_rows, padded),
            buffer(wide_rows, padded),
            buffer(wide_rows, padded),
            buffer(1, wide_rows, padded),
            buffer(3, wide_rows, padded),
            buffer(4, rows, cols),
            buffer(2, 3, 3 * rows),
            buffer(2, 4, 3 * rows),
            buffer(2, 1, packed),
            buffer(2, 3, packed),
            buffer(3, REACH, cols),
            buffer(2, 3, 3 * rows),
            buffer(2, 3, 16),
            buffer(4, REACH, cols),
            buffer(2, 4, 3 * rows),
            buffer(2, 4, 16),
            buffer(STEPS, 2, 1, REACH, padded),
            buffer(STEPS, 2, 1, packed),
            buffer(STEPS, 4, 1, 24),
            buffer(STEPS, 2, 3, REACH, padded),
            buffer(STEPS, 2, 3, packed),
            buffer(STEPS, 4, 3, 24),
            pltpu.SemaphoreType.DMA((7,)),
            pltpu.SemaphoreType.DMA((stages, 12)),
            pltpu.SemaphoreType.DMA((stages, 12)),
        ],
        compiler_params=pltpu.CompilerParams(
            collective_id=0, has_side_effects=True, vmem_limit_bytes=67_043_328
        ),
        name="peridynamics",
    )(displacement, velocity, intact, material, bulk_modulus, shear_modulus, density)
    return pl.pallas_call(
        hand_over,
        out_shape=(own, own, own),
        in_specs=[vmem] * 3,
        out_specs=(vmem, vmem, vmem),
        name="hand_over",
    )(*results)


def solution(mesh):
    node = P(None, "gx", "gy", None)
    return jax.shard_map(
        on_device,
        mesh=mesh,
        in_specs=(node, node, node, P("gx", "gy", None), P(), P(), P()),
        out_specs=(node, node, node),
        check_vma=False,
    )
```

profile of v0, /device:TPU:0, one launch (start us, length us, event | category | flops | bytes accessed | tf_op | source)
XLA Modules:
  0.0 44.7 jit_solution(17494570835006328346)
XLA Ops:
  0.6 42.4 %peridynamics.1 = (f32[3,8,8,128]{3,2,1,0:T(8,128)}, f32[3,8,8,128]{3,2,1,0:T(8,128)}, f32[3,8,8,128]{3,2,1,0:T(8,128)}) custom-call(f32[3,8,8,128]{3,2,1,0:T(8,128)} %u_hbm.1, f32[3,8,8,128]{3,2,1,0:T(8,128)} %v_hbm.1, s32[61,8,8,128]{3,2,1,0:T(8,128)} %intact_hbm.1, s32[8,8,128]{2,1,0:T(8,128)} %mat_hbm.1, f32[8]{0:T(128)} %bulk_hbm.1, f32[8]{0:T(128)} %shear_hbm.1, ...), custom_call_target="tpu_custom_call" | custom-call | tf_op jit(solution)/shard_map/peridynamics/pallas_call | solution.py:595
  43.0 1.7 %hand_over.1 = (f32[3,8,8,128]{3,2,1,0:T(8,128)}, f32[3,8,8,128]{3,2,1,0:T(8,128)}, f32[3,8,8,128]{3,2,1,0:T(8,128)}) custom-call(f32[3,8,8,128]{3,2,1,0:T(8,128)} %get-tuple-element.6.u_in, f32[3,8,8,128]{3,2,1,0:T(8,128)} %get-tuple-element.7.v_in, f32[3,8,8,128]{3,2,1,0:T(8,128)} %get-tuple-element.8.f_in), custom_call_target="tpu_custom_call" | custom-call | tf_op jit(solution)/shard_map/hand_over/pallas_call | solution.py:645
where the time goes:
time: 44.9 us; the launch traced here: 44.7 us
  Pallas kernels  44.1 us (98%)
  between operations  0.64 us (1%)
    pallas_call x1, Pallas kernels, on_device(): pl.pallas_call(functools.partial(kernel, lax.axis_size('gx'), lax.axis_si...  42.4 us
    pallas_call x1, Pallas kernels, on_device(): pl.pallas_call(hand_over, out_shape=(own, own, own), in_specs=[vmem] * 3,...  1.7 us

commit v1 on v0

v1 whole, which is shorter than its diff:
```python
import functools
import math

import jax
import jax.numpy as jnp
from jax import lax
from jax.experimental import pallas as pl
from jax.experimental.pallas import tpu as pltpu
from jax.sharding import PartitionSpec as P

STEPS = 2
TIME_STEP = 0.02
REACH = 3
NEAR = 2
MESH = pl.DeviceIdType.MESH
F32 = jnp.float32

AROUND = [(dx, dy) for dx in (-1, 0, 1) for dy in (-1, 0, 1) if (dx, dy) != (0, 0)]
STATE = [("S", (-1, 0)), ("S", (0, -1)), ("S", (0, 1)), ("S", (-1, -1)), ("S", (-1, 1))]
CHUNKS = {
    "C": [("C", (1, -1)), ("C", (1, 1)), ("C", (0, -1)), ("C", (0, 1)), ("C", (1, 0))],
    "A": [("A", (-1, -1)), ("A", (-1, 1)), ("A", (0, -1)), ("A", (0, 1)), ("A", (-1, 0))],
    "B": [("B", (0, -1)), ("B", (0, 1))],
}
FINAL = {
    "C": [("C", (1, -1)), ("C", (1, 1)), ("C", (1, 0))],
    "A": [("A", (0, -1)), ("A", (0, 1))],
    "B": [("B", (0, -1)), ("B", (0, 1))],
}
SLOT = {key: n for n, key in enumerate(CHUNKS["C"] + CHUNKS["A"] + CHUNKS["B"])}
SLOT.update({key: n for n, key in enumerate(STATE)})


def half_offsets():
    span = range(-REACH, REACH + 1)
    return [
        (a, b, c)
        for a in span
        for b in span
        for c in span
        if a * a + b * b + c * c <= REACH * REACH and (a, b, c) > (0, 0, 0)
    ]


OFFSETS = half_offsets()
GROUPS = {}
for _k, (_a, _b, _c) in enumerate(OFFSETS):
    GROUPS.setdefault((_a, _b), []).append((_k, _c))
RADII = [math.sqrt(float(a * a + b * b + c * c)) for a, b, c in OFFSETS]
VOLUME = 2.0 * sum(RADII)


def round_up(value, unit):
    return -(-value // unit) * unit


def spans(rows, cols, key, kind):
    chunk, (dx, dy) = key
    own = {(r, c) for r in range(rows) for c in range(cols)}
    wide = own | {(r + a, c + b) for r, c in own for a, b in GROUPS}
    sender = own if kind == "state" else wide
    receiver = own if kind == "final" else wide
    first, end = {
        "A": (0, REACH), "B": (REACH, rows), "C": (rows, rows + REACH), "S": (0, rows)
    }[chunk]
    runs = []
    for row in range(first, end):
        used = [c for r, c in sender if r == row and (r - dx * rows, c - dy * cols) in receiver]
        if used:
            runs.append((row, min(used), max(used) + 1 - min(used)))
    return runs


def stages():
    listed = [("u", "state", 3), ("m", "state", 1), ("v", "state", 3)]
    for step in range(STEPS):
        listed.append((("t", step), "sum", 1))
        listed.append((("f", step), "final" if step == STEPS - 1 else "sum", 3))
    return listed


def keys_of(kind):
    if kind == "state":
        return STATE
    chunks = FINAL if kind == "final" else CHUNKS
    return chunks["C"] + chunks["A"] + chunks["B"]


def layout(rows, cols):
    place, at = {}, 0
    for number, (_, kind, comps) in enumerate(stages()):
        for key in keys_of(kind):
            if key[1][1] == 0:
                continue
            runs = spans(rows, cols, key, kind)
            size = round_up(comps * sum(width for _, _, width in runs), 8)
            place[number, key] = (at, size, runs)
            at += size
    return place, at


def tree_sum(terms):
    while len(terms) > 1:
        terms = [
            terms[n] + terms[n + 1] if n + 1 < len(terms) else terms[n]
            for n in range(0, len(terms), 2)
        ]
    return terms[0]


def kernel(
    grid_rows,
    grid_cols,
    u_hbm,
    v_hbm,
    intact_hbm,
    mat_hbm,
    bulk_hbm,
    shear_hbm,
    dens_hbm,
    out_u,
    out_v,
    out_f,
    u_ref,
    v_ref,
    mat_ref,
    mat_f32,
    bulk_ref,
    shear_ref,
    dens_ref,
    intact_ref,
    flag,
    by_inverse,
    by_stretch,
    wide_u,
    wide_v,
    wide_m,
    u_shift,
    a_shift,
    b_shift,
    a_coef,
    inertia,
    strain,
    force,
    send_buf,
    recv_buf,
    u_slab,
    m_slab,
    v_slab,
    t_slab,
    f_slab,
    local_sem,
    send_sem,
    recv_sem,
):
    rows, cols, nz = mat_ref.shape
    wide_rows = rows + REACH
    gx = lax.axis_index("gx")
    gy = lax.axis_index("gy")
    place, _ = layout(rows, cols)
    listed = stages()
    number_of = {name: number for number, (name, _, _) in enumerate(listed)}

    def present(direction):
        x = gx + direction[0]
        y = gy + direction[1]
        return (x >= 0) & (x < grid_rows) & (y >= 0) & (y < grid_cols)

    here = {direction: present(direction) for direction in AROUND}

    barrier = pltpu.get_barrier_semaphore()
    for direction in AROUND:

        @pl.when(here[direction])
        def _(direction=direction):
            pl.semaphore_signal(
                barrier,
                inc=1,
                device_id=(gx + direction[0], gy + direction[1]),
                device_id_type=MESH,
            )

    loads = [
        pltpu.make_async_copy(source, target, local_sem.at[n])
        for n, (source, target) in enumerate(
            [
                (u_hbm, u_ref),
                (v_hbm, v_ref),
                (mat_hbm, mat_ref),
                (intact_hbm, intact_ref),
                (bulk_hbm, bulk_ref),
                (shear_hbm, shear_ref),
                (dens_hbm, dens_ref),
            ]
        )
    ]
    for load in loads:
        load.start()

    def side(value):
        return 0 if value < 0 else 1

    def slab(name, key):
        if name == "u":
            return u_slab
        if name == "m":
            return m_slab
        if name == "v":
            return v_slab
        buf = t_slab if name[0] == "t" else f_slab
        return buf.at[name[1], side(-key[1][0])]

    def ends(name, key, whole):
        number = number_of[name]
        if key[1][1] == 0:
            first = rows if key[0] == "C" else 0
            return whole.at[:, first : first + REACH], slab(name, key)
        at, size, _ = place[number, key]
        return send_buf.at[at : at + size], recv_buf.at[at : at + size]

    def copy_to(name, key, whole):
        dx, dy = key[1]
        source, target = ends(name, key, whole)
        return pltpu.make_async_remote_copy(
            src_ref=source,
            dst_ref=target,
            send_sem=send_sem.at[number_of[name], SLOT[key]],
            recv_sem=recv_sem.at[number_of[name], SLOT[key]],
            device_id=(gx + dx, gy + dy),
            device_id_type=MESH,
        )

    def pack(name, keys, whole, first_col):
        number = number_of[name]
        comps = listed[number][2]
        for key in keys:
            if key[1][1] == 0:
                continue
            at, _, runs = place[number, key]
            for comp in range(comps):
                for row, col, width in runs:
                    begin = first_col + col
                    send_buf[at : at + width] = whole[comp, row, begin : begin + width]
                    at += width

    def start_all(name, keys, whole):
        for key in keys:

            @pl.when(here[key[1]])
            def _(key=key):
                copy_to(name, key, whole).start()

    def wait_recv(name, key, whole):
        _, target = ends(name, key, whole)
        pltpu.make_async_remote_copy(
            src_ref=target,
            dst_ref=target,
            send_sem=send_sem.at[number_of[name], SLOT[key]],
            recv_sem=recv_sem.at[number_of[name], SLOT[key]],
            device_id=(gx - key[1][0], gy - key[1][1]),
            device_id_type=MESH,
        ).wait_recv()

    def wait_sends(name, keys, whole):
        for key in keys:

            @pl.when(here[key[1]])
            def _(key=key):
                copy_to(name, key, whole).wait_send()

    def landed(name, key):
        number = number_of[name]
        at, _, runs = place[number, key]
        dx, dy = key[1]
        for comp in range(listed[number][2]):
            for row, col, width in runs:
                yield comp, row - dx * rows, REACH + col - dy * cols, at, width
                at += width

    def take_state(name, own, wide):
        for key in STATE:
            origin = (-key[1][0], -key[1][1])

            @pl.when(here[origin])
            def _(key=key, origin=origin):
                wait_recv(name, key, own)
                if origin[1] == 0:
                    buf = slab(name, key)
                    for comp in range(own.shape[0]):
                        for r in range(REACH):
                            wide[comp, rows + r, REACH : REACH + cols] = buf[comp, r]
                    return
                for comp, row, col, at, width in landed(name, key):
                    wide[comp, row, col : col + width] = recv_buf[at : at + width]

    def take_sums(name, keys, whole):
        comps = whole.shape[0]
        wait_sends(name, [key for key in keys if key[1][1] == 0], whole)
        for key in keys:
            origin = (-key[1][0], -key[1][1])

            @pl.when(here[origin])
            def _(key=key, origin=origin):
                wait_recv(name, key, whole)
                if origin[1] == 0:
                    buf = slab(name, key)
                    first = (rows if key[0] == "C" else 0) + origin[0] * rows
                    for comp in range(comps):
                        for n in range(REACH):
                            whole[comp, first + n] = whole[comp, first + n] + buf[comp, n]
                    return
                for comp, row, col, at, width in landed(name, key):
                    span = slice(col, col + width)
                    whole[comp, row, span] = whole[comp, row, span] + recv_buf[at : at + width]

    loads[0].wait()
    pack("u", STATE, u_ref, 0)

    on_x = (gx > 0).astype(jnp.int32) + (gx < grid_rows - 1).astype(jnp.int32)
    on_y = (gy > 0).astype(jnp.int32) + (gy < grid_cols - 1).astype(jnp.int32)
    pl.semaphore_wait(barrier, (1 + on_x) * (1 + on_y) - 1)
    start_all("u", STATE, u_ref)

    loads[1].wait()
    loads[2].wait()
    mat_f32[0] = mat_ref[...].astype(F32)
    pack("m", STATE, mat_f32, 0)
    pack("v", STATE, v_ref, 0)

    wide_u[...] = jnp.zeros(wide_u.shape, F32)
    wide_v[...] = jnp.zeros(wide_v.shape, F32)
    wide_m[...] = jnp.zeros(wide_m.shape, F32)
    for comp in range(3):
        wide_u[comp, 0:rows, REACH : REACH + cols] = u_ref[comp]
        wide_v[comp, 0:rows, REACH : REACH + cols] = v_ref[comp]
    wide_m[0, 0:rows, REACH : REACH + cols] = mat_f32[0]

    def shifted(values, c):
        if c == 0:
            return values
        lane = lax.broadcasted_iota(jnp.int32, values.shape, 1)
        moved = pltpu.roll(values, (-c) % nz, axis=1)
        return jnp.where((lane + c >= 0) & (lane + c < nz), moved, 0.0)

    def shift_motion():
        for r in range(wide_rows):
            for comp in range(3):
                values = wide_u[comp, r]
                for c in range(-NEAR, NEAR + 1):
                    moved = shifted(values, c)
                    if comp == 2 and c != 0:
                        moved = moved + float(c)
                    u_shift[c + NEAR, comp, r] = moved

    def materials():
        for r in range(wide_rows):
            classes = wide_m[0, r]
            bulk = jnp.full(classes.shape, bulk_ref[0], F32)
            shear = jnp.full(classes.shape, shear_ref[0], F32)
            dens = jnp.full(classes.shape, dens_ref[0], F32)
            for number in range(1, bulk_ref.shape[0]):
                match = classes == float(number)
                bulk = jnp.where(match, bulk_ref[number], bulk)
                shear = jnp.where(match, shear_ref[number], shear)
                dens = jnp.where(match, dens_ref[number], dens)
            inertia[r] = TIME_STEP / dens
            a_coef[r] = (9.0 / (VOLUME * VOLUME)) * (bulk - (5.0 / 3.0) * shear)
            stiff = (15.0 / VOLUME) * shear
            for c in range(-NEAR, NEAR + 1):
                b_shift[c + NEAR, r] = shifted(stiff, c)

    depth = lax.broadcasted_iota(jnp.int32, (cols, nz), 1)
    column = lax.broadcasted_iota(jnp.int32, (cols, nz), 0) + gy * cols

    def partner(buffer, i, a, b, c, own):
        if c > NEAR:
            return shifted(own, c)
        return buffer[c + NEAR, i + a, pl.ds(REACH + b, cols)]

    def bond_vector(i, a, b, c, own):
        y = []
        for comp in range(3):
            if c > NEAR:
                there = shifted(own[3][comp], c)
                if comp == 2:
                    there = there + float(c)
            else:
                there = u_shift[c + NEAR, comp, i + a, pl.ds(REACH + b, cols)]
            y.append(there - (own[0][a], own[1][b], own[2])[comp])
        return y

    def geometry(i, a, b, c, own):
        y0, y1, y2 = bond_vector(i, a, b, c, own)
        square = y0 * y0 + y1 * y1 + y2 * y2
        inverse = lax.rsqrt(square)
        return square * inverse, inverse

    def own_motion(i):
        mine = [wide_u[comp, i, REACH : REACH + cols] for comp in range(3)]
        by_row = {a: mine[0] - float(a) for a in range(REACH + 1)}
        by_col = {b: mine[1] - float(b) for b in range(-REACH, REACH + 1)}
        return (by_row, by_col, mine[2], mine)

    def back(values, c):
        return values if c == 0 else pltpu.roll(values, c % nz, axis=1)

    def order(t):
        return lax.rem(t + rows - REACH, rows)

    def send_done(t, name, keys, whole):
        @pl.when(t == REACH - 1)
        def _():
            pack(name, keys["C"], whole, REACH)
            start_all(name, keys["C"], whole)

        @pl.when(t == 2 * REACH - 1)
        def _():
            pack(name, keys["A"], whole, REACH)
            start_all(name, keys["A"], whole)

    def weights():
        @pl.loop(0, rows)
        def _(i):
            lane_in = {
                c: jnp.where((depth + c >= 0) & (depth + c < nz), 1.0, 0.0)
                for c in range(-NEAR, REACH + 1)
            }
            for (a, b), members in GROUPS.items():
                row_in = (gx * rows + i + a) < grid_rows * rows
                plane = jnp.where(
                    (column + b >= 0) & (column + b < grid_cols * cols) & row_in, 1.0, 0.0
                )
                for k, c in members:
                    flag[k, i] = intact_ref[k, i].astype(F32) * (plane * lane_in[c])

    def prepare():
        @pl.loop(0, rows)
        def _(i):
            own_b = b_shift[NEAR, i, pl.ds(REACH, cols)]
            for k, (a, b, c) in enumerate(OFFSETS):
                both_b = own_b + partner(b_shift, i, a, b, c, own_b)
                scale = flag[k, i] * by_inverse[k, i]
                by_stretch[k, i] = scale * (both_b * (by_stretch[k, i] * (1.0 / RADII[k])))
                by_inverse[k, i] = scale

    def strain_pass(send):
        strain[...] = jnp.zeros(strain.shape, F32)

        @pl.loop(0, rows)
        def _(t):
            i = order(t)
            own = own_motion(i)
            sums = []
            for (a, b), members in GROUPS.items():
                returned = []
                for k, c in members:
                    length, inverse = geometry(i, a, b, c, own)
                    stretch = length - RADII[k]
                    by_inverse[k, i] = inverse
                    by_stretch[k, i] = stretch
                    term = flag[k, i] * stretch
                    sums.append(term)
                    returned.append(back(term, c))
                at = pl.ds(REACH + b, cols)
                strain[0, i + a, at] = strain[0, i + a, at] + tree_sum(returned)
                sums = [tree_sum(sums)]
            at = pl.ds(REACH, cols)
            strain[0, i, at] = strain[0, i, at] + sums[0]
            send(t)

    def force_pass(send):
        force[...] = jnp.zeros(force.shape, F32)

        @pl.loop(0, rows)
        def _(t):
            i = order(t)
            own = own_motion(i)
            mid = pl.ds(REACH, cols)
            own_a = a_shift[NEAR, i, mid]
            sums = [[], [], []]
            for (a, b), members in GROUPS.items():
                at = pl.ds(REACH + b, cols)
                returned = [[], [], []]
                for k, c in members:
                    y = bond_vector(i, a, b, c, own)
                    both_a = own_a + partner(a_shift, i, a, b, c, own_a)
                    tension = by_inverse[k, i] * both_a + by_stretch[k, i]
                    for comp in range(3):
                        term = tension * y[comp]
                        sums[comp].append(term)
                        returned[comp].append(back(term, c))
                for comp in range(3):
                    force[comp, i + a, at] = force[comp, i + a, at] - tree_sum(returned[comp])
                    sums[comp] = [tree_sum(sums[comp])]
            for comp in range(3):
                force[comp, i, mid] = force[comp, i, mid] + sums[comp][0]

            send(t)

    for load in loads[3:]:
        load.wait()
    weights()
    take_state("u", u_ref, wide_u)
    start_all("m", STATE, mat_f32)
    shift_motion()

    for step in range(STEPS):
        last = step == STEPS - 1
        name = ("t", step)
        every = keys_of("sum")
        strain_pass(lambda t, name=name: send_done(t, name, CHUNKS, strain))
        pack(name, CHUNKS["B"], strain, REACH)
        start_all(name, CHUNKS["B"], strain)
        if step == 0:
            start_all("v", STATE, v_ref)
            take_state("m", mat_f32, wide_m)
            materials()
        prepare()
        take_sums(name, every, strain)

        for r in range(wide_rows):
            values = strain[0, r] * a_coef[r]
            for c in range(-NEAR, NEAR + 1):
                a_shift[c + NEAR, r] = shifted(values, c)

        wait_sends(name, [key for key in every if key[1][1] != 0], strain)
        name = ("f", step)
        keys = FINAL if last else CHUNKS
        every = keys_of("final" if last else "sum")
        force_pass(lambda t, name=name, keys=keys: send_done(t, name, keys, force))
        pack(name, keys["B"], force, REACH)
        start_all(name, keys["B"], force)
        if step == 0:
            take_state("v", v_ref, wide_v)
        take_sums(name, every, force)
        if not last:
            for r in range(wide_rows):
                for comp in range(3):
                    speed = wide_v[comp, r] + force[comp, r] * inertia[r]
                    wide_v[comp, r] = speed
                    wide_u[comp, r] = wide_u[comp, r] + TIME_STEP * speed

            shift_motion()
        else:
            mid = pl.ds(REACH, cols)
            for r in range(rows):
                for comp in range(3):
                    pull = force[comp, r, mid]
                    speed = wide_v[comp, r, mid] + pull * inertia[r, mid]
                    out_f[comp, r] = pull
                    out_v[comp, r] = speed
                    out_u[comp, r] = wide_u[comp, r, mid] + TIME_STEP * speed

        wait_sends(name, [key for key in every if key[1][1] != 0], force)
    for name, own in (("u", u_ref), ("m", mat_f32), ("v", v_ref)):
        wait_sends(name, STATE, own)


def hand_over(u_in, v_in, f_in, u_out, v_out, f_out):
    u_out[...] = u_in[...]
    v_out[...] = v_in[...]
    f_out[...] = f_in[...]


def on_device(displacement, velocity, intact, material, bulk_modulus, shear_modulus, density):
    rows, cols, nz = material.shape
    wide_rows = rows + REACH
    padded = round_up(cols + 2 * REACH, 8)
    packed = layout(rows, cols)[1]
    own = jax.ShapeDtypeStruct((3, rows, cols, nz), F32)
    vmem = pl.BlockSpec(memory_space=pltpu.VMEM)
    hbm = pl.BlockSpec(memory_space=pltpu.HBM)
    table = pltpu.SMEM(bulk_modulus.shape, F32)

    def buffer(*shape):
        return pltpu.VMEM(shape + (nz,), F32)

    results = pl.pallas_call(
        functools.partial(kernel, lax.axis_size("gx"), lax.axis_size("gy")),
        out_shape=(own, own, own),
        in_specs=[hbm] * 7,
        out_specs=(vmem, vmem, vmem),
        scratch_shapes=[
            buffer(3, rows, cols),
            buffer(3, rows, cols),
            pltpu.VMEM(material.shape, jnp.int32),
            buffer(1, rows, cols),
            table,
            table,
            table,
            pltpu.VMEM(intact.shape, jnp.int32),
            pltpu.VMEM(intact.shape, F32),
            pltpu.VMEM(intact.shape, F32),
            pltpu.VMEM(intact.shape, F32),
            buffer(3, wide_rows, padded),
            buffer(3, wide_rows, padded),
            buffer(1, wide_rows, padded),
            buffer(5, 3, wide_rows, padded),
            buffer(5, wide_rows, padded),
            buffer(5, wide_rows, padded),
            buffer(wide_rows, padded),
            buffer(wide_rows, padded),
            buffer(1, wide_rows, padded),
            buffer(3, wide_rows, padded),
            buffer(packed),
            buffer(packed),
            buffer(3, REACH, cols),
            buffer(1, REACH, cols),
            buffer(3, REACH, cols),
            buffer(STEPS, 2, 1, REACH, padded),
            buffer(STEPS, 2, 3, REACH, padded),
            pltpu.SemaphoreType.DMA((7,)),
            pltpu.SemaphoreType.DMA((len(stages()), 12)),
            pltpu.SemaphoreType.DMA((len(stages()), 12)),
        ],
        compiler_params=pltpu.CompilerParams(
            collective_id=0, has_side_effects=True, vmem_limit_bytes=67_043_328
        ),
        name="peridynamics",
    )(displacement, velocity, intact, material, bulk_modulus, shear_modulus, density)
    return pl.pallas_call(
        hand_over,
        out_shape=(own, own, own),
        in_specs=[vmem] * 3,
        out_specs=(vmem, vmem, vmem),
        name="hand_over",
    )(*results)


def solution(mesh):
    node = P(None, "gx", "gy", None)
    return jax.shard_map(
        on_device,
        mesh=mesh,
        in_specs=(node, node, node, P("gx", "gy", None), P(), P(), P()),
        out_specs=(node, node, node),
        check_vma=False,
    )
```

time: 44.9 us -> 36.7 us (0.82)
  Pallas kernels: 44.1 us -> 35.9 us
    pallas_call x1, Pallas kernels: 42.4 us -> 34.2 us  [on_device(): pl.pallas_call(functools.partial(kernel, lax.axis_size('gx'), lax.axis_si...]
where the time goes in v1:
time: 36.7 us; the launch traced here: 36.5 us
  Pallas kernels  35.9 us (98%)
  between operations  0.64 us (2%)
    pallas_call x1, Pallas kernels, on_device(): pl.pallas_call(functools.partial(kernel, lax.axis_size('gx'), lax.axis_si...  34.2 us
    pallas_call x1, Pallas kernels, on_device(): pl.pallas_call(hand_over, out_shape=(own, own, own), in_specs=[vmem] * 3,...  1.7 us

profile of v1, /device:TPU:0, one launch (start us, length us, event | category | flops | bytes accessed | tf_op | source)
XLA Modules:
  0.0 36.5 jit_solution(13542640589544696078)
XLA Ops:
  0.6 34.2 %peridynamics.1 = (f32[3,8,8,128]{3,2,1,0:T(8,128)}, f32[3,8,8,128]{3,2,1,0:T(8,128)}, f32[3,8,8,128]{3,2,1,0:T(8,128)}) custom-call(f32[3,8,8,128]{3,2,1,0:T(8,128)} %u_hbm.1, f32[3,8,8,128]{3,2,1,0:T(8,128)} %v_hbm.1, s32[61,8,8,128]{3,2,1,0:T(8,128)} %intact_hbm.1, s32[8,8,128]{2,1,0:T(8,128)} %mat_hbm.1, f32[8]{0:T(128)} %bulk_hbm.1, f32[8]{0:T(128)} %shear_hbm.1, ...), custom_call_target="tpu_custom_call" | custom-call | tf_op jit(solution)/shard_map/peridynamics/pallas_call | solution.py:578
  34.8 1.7 %hand_over.1 = (f32[3,8,8,128]{3,2,1,0:T(8,128)}, f32[3,8,8,128]{3,2,1,0:T(8,128)}, f32[3,8,8,128]{3,2,1,0:T(8,128)}) custom-call(f32[3,8,8,128]{3,2,1,0:T(8,128)} %get-tuple-element.6.u_in, f32[3,8,8,128]{3,2,1,0:T(8,128)} %get-tuple-element.7.v_in, f32[3,8,8,128]{3,2,1,0:T(8,128)} %get-tuple-element.8.f_in), custom_call_target="tpu_custom_call" | custom-call | tf_op jit(solution)/shard_map/hand_over/pallas_call | solution.py:621

commit v2 on v1

--- a/solution.py
+++ b/solution.py
@@ -52,6 +52,23 @@
 
 def round_up(value, unit):
     return -(-value // unit) * unit
+
+
+AT_PARTNER = [(1, -1), (1, 1), (2, -1), (2, 1)]
+
+
+def bond_order(rows):
+    tail = range(rows - REACH, rows)
+    groups = list(GROUPS)
+    return [
+        ("C", [(i, [(a, b) for a, b in groups if i + a >= rows]) for i in tail]),
+        ("A", [(i, groups) for i in range(REACH)]),
+        (
+            "B",
+            [(i, groups) for i in range(REACH, rows - REACH)]
+            + [(i, [(a, b) for a, b in groups if i + a < rows]) for i in tail],
+        ),
+    ]
 
 
 def spans(rows, cols, key, kind):
@@ -404,19 +421,9 @@
     def back(values, c):
         return values if c == 0 else pltpu.roll(values, c % nz, axis=1)
 
-    def order(t):
-        return lax.rem(t + rows - REACH, rows)
-
-    def send_done(t, name, keys, whole):
-        @pl.when(t == REACH - 1)
-        def _():
-            pack(name, keys["C"], whole, REACH)
-            start_all(name, keys["C"], whole)
-
-        @pl.when(t == 2 * REACH - 1)
-        def _():
-            pack(name, keys["A"], whole, REACH)
-            start_all(name, keys["A"], whole)
+    def send_done(name, chunk, keys, whole):
+        pack(name, keys[chunk], whole, REACH)
+        start_all(name, keys[chunk], whole)
 
     def weights():
         @pl.loop(0, rows)
@@ -445,57 +452,75 @@
 
     def strain_pass(send):
         strain[...] = jnp.zeros(strain.shape, F32)
-
-        @pl.loop(0, rows)
-        def _(t):
-            i = order(t)
-            own = own_motion(i)
-            sums = []
-            for (a, b), members in GROUPS.items():
-                returned = []
-                for k, c in members:
-                    length, inverse = geometry(i, a, b, c, own)
-                    stretch = length - RADII[k]
-                    by_inverse[k, i] = inverse
-                    by_stretch[k, i] = stretch
-                    term = flag[k, i] * stretch
-                    sums.append(term)
-                    returned.append(back(term, c))
-                at = pl.ds(REACH + b, cols)
-                strain[0, i + a, at] = strain[0, i + a, at] + tree_sum(returned)
-                sums = [tree_sum(sums)]
-            at = pl.ds(REACH, cols)
-            strain[0, i, at] = strain[0, i, at] + sums[0]
-            send(t)
+        mid = pl.ds(REACH, cols)
+        for chunk, work in bond_order(rows):
+            for i, groups in work:
+                own = own_motion(i)
+                sums = []
+                for a, b in groups:
+                    returned = []
+                    for k, c in GROUPS[a, b]:
+                        length, inverse = geometry(i, a, b, c, own)
+                        stretch = length - RADII[k]
+                        by_inverse[k, i] = inverse
+                        by_stretch[k, i] = stretch
+                        term = flag[k, i] * stretch
+                        sums.append(term)
+                        returned.append(back(term, c))
+                    at = pl.ds(REACH + b, cols)
+                    strain[0, i + a, at] = strain[0, i + a, at] + tree_sum(returned)
+                    sums = [tree_sum(sums)]
+                strain[0, i, mid] = strain[0, i, mid] + sums[0]
+            send(chunk)
 
     def force_pass(send):
         force[...] = jnp.zeros(force.shape, F32)
-
-        @pl.loop(0, rows)
-        def _(t):
-            i = order(t)
-            own = own_motion(i)
-            mid = pl.ds(REACH, cols)
-            own_a = a_shift[NEAR, i, mid]
-            sums = [[], [], []]
-            for (a, b), members in GROUPS.items():
-                at = pl.ds(REACH + b, cols)
-                returned = [[], [], []]
-                for k, c in members:
-                    y = bond_vector(i, a, b, c, own)
-                    both_a = own_a + partner(a_shift, i, a, b, c, own_a)
-                    tension = by_inverse[k, i] * both_a + by_stretch[k, i]
-                    for comp in range(3):
-                        term = tension * y[comp]
-                        sums[comp].append(term)
-                        returned[comp].append(back(term, c))
+        mid = pl.ds(REACH, cols)
+        for chunk, work in bond_order(rows):
+            for i, groups in work:
+                own = own_motion(i)
+                own_a = a_shift[NEAR, i, mid]
+                sums = [[], [], []]
+                for a, b in groups:
+                    at = pl.ds(REACH + b, cols)
+                    tensions = []
+                    for k, c in GROUPS[a, b]:
+                        both_a = own_a + partner(a_shift, i, a, b, c, own_a)
+                        tensions.append((c, by_inverse[k, i] * both_a + by_stretch[k, i]))
+                    if (a, b) in AT_PARTNER:
+                        base = (own[0][a], own[1][b], own[2])
+                        shift = (float(a), float(b), 0.0)
+                        pulled = [(c, back(tension, c)) for c, tension in tensions]
+                        here_all = tree_sum([tension for _, tension in tensions])
+                        there_all = tree_sum([tension for _, tension in pulled])
+                        for comp in range(3):
+                            direct = tree_sum(
+                                [t * u_shift[c + NEAR, comp, i + a, at] for c, t in tensions]
+                            )
+                            sums[comp].append(direct - base[comp] * here_all)
+                            origin = tree_sum(
+                                [t * u_shift[NEAR - c, comp, i, mid] for c, t in pulled]
+                            )
+                            end = u_shift[NEAR, comp, i + a, at] + shift[comp]
+                            force[comp, i + a, at] = force[comp, i + a, at] + (
+                                origin - end * there_all
+                            )
+                    else:
+                        returned = [[], [], []]
+                        for c, tension in tensions:
+                            y = bond_vector(i, a, b, c, own)
+                            for comp in range(3):
+                                term = tension * y[comp]
+                                sums[comp].append(term)
+                                returned[comp].append(back(term, c))
+                        for comp in range(3):
+                            force[comp, i + a, at] = force[comp, i + a, at] - tree_sum(
+                                returned[comp]
+                            )
+                    sums = [[tree_sum(sums[comp])] for comp in range(3)]
                 for comp in range(3):
-                    force[comp, i + a, at] = force[comp, i + a, at] - tree_sum(returned[comp])
-                    sums[comp] = [tree_sum(sums[comp])]
-            for comp in range(3):
-                force[comp, i, mid] = force[comp, i, mid] + sums[comp][0]
-
-            send(t)
+                    force[comp, i, mid] = force[comp, i, mid] + sums[comp][0]
+            send(chunk)
 
     for load in loads[3:]:
         load.wait()
@@ -508,9 +533,7 @@
         last = step == STEPS - 1
         name = ("t", step)
         every = keys_of("sum")
-        strain_pass(lambda t, name=name: send_done(t, name, CHUNKS, strain))
-        pack(name, CHUNKS["B"], strain, REACH)
-        start_all(name, CHUNKS["B"], strain)
+        strain_pass(lambda chunk, name=name: send_done(name, chunk, CHUNKS, strain))
         if step == 0:
             start_all("v", STATE, v_ref)
             take_state("m", mat_f32, wide_m)
@@ -527,9 +550,7 @@
         name = ("f", step)
         keys = FINAL if last else CHUNKS
         every = keys_of("final" if last else "sum")
-        force_pass(lambda t, name=name, keys=keys: send_done(t, name, keys, force))
-        pack(name, keys["B"], force, REACH)
-        start_all(name, keys["B"], force)
+        force_pass(lambda chunk, name=name, keys=keys: send_done(name, chunk, keys, force))
         if step == 0:
             take_state("v", v_ref, wide_v)
         take_sums(name, every, force)

time: 36.7 us -> 34.8 us (0.948)
  Pallas kernels: 35.9 us -> 34 us
    pallas_call x1, Pallas kernels: 34.2 us -> 32.3 us  [on_device(): pl.pallas_call(functools.partial(kernel, lax.axis_size('gx'), lax.axis_si...]
where the time goes in v2:
time: 34.8 us; the launch traced here: 34.7 us
  Pallas kernels  34 us (98%)
  between operations  0.64 us (2%)
    pallas_call x1, Pallas kernels, on_device(): pl.pallas_call(functools.partial(kernel, lax.axis_size('gx'), lax.axis_si...  32.3 us
    pallas_call x1, Pallas kernels, on_device(): pl.pallas_call(hand_over, out_shape=(own, own, own), in_specs=[vmem] * 3,...  1.7 us

profile of v2, /device:TPU:0, one launch (start us, length us, event | category | flops | bytes accessed | tf_op | source)
XLA Modules:
  0.0 34.7 jit_solution(13811575827130102030)
XLA Ops:
  0.6 32.3 %peridynamics.1 = (f32[3,8,8,128]{3,2,1,0:T(8,128)}, f32[3,8,8,128]{3,2,1,0:T(8,128)}, f32[3,8,8,128]{3,2,1,0:T(8,128)}) custom-call(f32[3,8,8,128]{3,2,1,0:T(8,128)} %u_hbm.1, f32[3,8,8,128]{3,2,1,0:T(8,128)} %v_hbm.1, s32[61,8,8,128]{3,2,1,0:T(8,128)} %intact_hbm.1, s32[8,8,128]{2,1,0:T(8,128)} %mat_hbm.1, f32[8]{0:T(128)} %bulk_hbm.1, f32[8]{0:T(128)} %shear_hbm.1, ...), custom_call_target="tpu_custom_call" | custom-call | tf_op jit(solution)/shard_map/peridynamics/pallas_call | solution.py:599
  33.0 1.7 %hand_over.1 = (f32[3,8,8,128]{3,2,1,0:T(8,128)}, f32[3,8,8,128]{3,2,1,0:T(8,128)}, f32[3,8,8,128]{3,2,1,0:T(8,128)}) custom-call(f32[3,8,8,128]{3,2,1,0:T(8,128)} %get-tuple-element.6.u_in, f32[3,8,8,128]{3,2,1,0:T(8,128)} %get-tuple-element.7.v_in, f32[3,8,8,128]{3,2,1,0:T(8,128)} %get-tuple-element.8.f_in), custom_call_target="tpu_custom_call" | custom-call | tf_op jit(solution)/shard_map/hand_over/pallas_call | solution.py:642

commit v3 on v2

--- a/solution.py
+++ b/solution.py
@@ -21,13 +21,25 @@
     "C": [("C", (1, -1)), ("C", (1, 1)), ("C", (0, -1)), ("C", (0, 1)), ("C", (1, 0))],
     "A": [("A", (-1, -1)), ("A", (-1, 1)), ("A", (0, -1)), ("A", (0, 1)), ("A", (-1, 0))],
     "B": [("B", (0, -1)), ("B", (0, 1))],
+    "E": [("E", (0, -1)), ("E", (0, 1))],
 }
 FINAL = {
     "C": [("C", (1, -1)), ("C", (1, 1)), ("C", (1, 0))],
     "A": [("A", (0, -1)), ("A", (0, 1))],
     "B": [("B", (0, -1)), ("B", (0, 1))],
+    "E": [("E", (0, -1)), ("E", (0, 1))],
 }
-SLOT = {key: n for n, key in enumerate(CHUNKS["C"] + CHUNKS["A"] + CHUNKS["B"])}
+CROSSED = {
+    "C": [("C", (1, 0))],
+    "A": [("A", (-1, 0))],
+    "B": [("B", (0, -1)), ("B", (0, 1))],
+    "E": [("E", (0, -1)), ("E", (0, 1))],
+    "A late": [("A", (0, -1)), ("A", (0, 1))],
+    "C late": [("C", (0, -1)), ("C", (0, 1))],
+}
+ORDERS = {"sum": CHUNKS, "final": FINAL, "crossed": CROSSED}
+SLOT = {key: n for n, key in enumerate(sum(CHUNKS.values(), []))}
+SLOTS = len(SLOT)
 SLOT.update({key: n for n, key in enumerate(STATE)})
 
 
@@ -54,21 +66,19 @@
     return -(-value // unit) * unit
 
 
-AT_PARTNER = [(1, -1), (1, 1), (2, -1), (2, 1)]
-
-
-def bond_order(rows):
+AT_PARTNER = [(a, b) for a in (1, 2) for b in (-2, -1, 1, 2)]
+
+
+def bond_order(rows, order):
     tail = range(rows - REACH, rows)
     groups = list(GROUPS)
-    return [
-        ("C", [(i, [(a, b) for a, b in groups if i + a >= rows]) for i in tail]),
-        ("A", [(i, groups) for i in range(REACH)]),
-        (
-            "B",
-            [(i, groups) for i in range(REACH, rows - REACH)]
-            + [(i, [(a, b) for a, b in groups if i + a < rows]) for i in tail],
-        ),
-    ]
+    work = {
+        "C": [(i, [(a, b) for a, b in groups if i + a >= rows]) for i in tail],
+        "A": [(i, groups) for i in range(REACH)],
+        "B": [(i, groups) for i in range(REACH, rows - REACH)],
+        "E": [(i, [(a, b) for a, b in groups if i + a < rows]) for i in tail],
+    }
+    return [(chunk, work[chunk]) for chunk in order]
 
 
 def spans(rows, cols, key, kind):
@@ -76,9 +86,15 @@
     own = {(r, c) for r in range(rows) for c in range(cols)}
     wide = own | {(r + a, c + b) for r, c in own for a, b in GROUPS}
     sender = own if kind == "state" else wide
+    if kind == "crossed":
+        sender = {(r + x, c) for r, c in wide for x in (-rows, 0, rows)}
     receiver = own if kind == "final" else wide
     first, end = {
-        "A": (0, REACH), "B": (REACH, rows), "C": (rows, rows + REACH), "S": (0, rows)
+        "A": (0, REACH),
+        "B": (REACH, rows - REACH),
+        "E": (rows - REACH, rows),
+        "C": (rows, rows + REACH),
+        "S": (0, rows),
     }[chunk]
     runs = []
     for row in range(first, end):
@@ -92,15 +108,14 @@
     listed = [("u", "state", 3), ("m", "state", 1), ("v", "state", 3)]
     for step in range(STEPS):
         listed.append((("t", step), "sum", 1))
-        listed.append((("f", step), "final" if step == STEPS - 1 else "sum", 3))
+        listed.append((("f", step), "final" if step == STEPS - 1 else "crossed", 3))
     return listed
 
 
 def keys_of(kind):
     if kind == "state":
         return STATE
-    chunks = FINAL if kind == "final" else CHUNKS
-    return chunks["C"] + chunks["A"] + chunks["B"]
+    return sum(ORDERS[kind].values(), [])
 
 
 def layout(rows, cols):
@@ -294,8 +309,8 @@
                 yield comp, row - dx * rows, REACH + col - dy * cols, at, width
                 at += width
 
-    def take_state(name, own, wide):
-        for key in STATE:
+    def take_state(name, keys, own, wide):
+        for key in keys:
             origin = (-key[1][0], -key[1][1])
 
             @pl.when(here[origin])
@@ -310,25 +325,47 @@
                 for comp, row, col, at, width in landed(name, key):
                     wide[comp, row, col : col + width] = recv_buf[at : at + width]
 
-    def take_sums(name, keys, whole):
-        comps = whole.shape[0]
-        wait_sends(name, [key for key in keys if key[1][1] == 0], whole)
-        for key in keys:
-            origin = (-key[1][0], -key[1][1])
-
-            @pl.when(here[origin])
-            def _(key=key, origin=origin):
-                wait_recv(name, key, whole)
-                if origin[1] == 0:
-                    buf = slab(name, key)
-                    first = (rows if key[0] == "C" else 0) + origin[0] * rows
-                    for comp in range(comps):
-                        for n in range(REACH):
-                            whole[comp, first + n] = whole[comp, first + n] + buf[comp, n]
-                    return
-                for comp, row, col, at, width in landed(name, key):
-                    span = slice(col, col + width)
-                    whole[comp, row, span] = whole[comp, row, span] + recv_buf[at : at + width]
+    def take_sum(name, key, whole):
+        origin = (-key[1][0], -key[1][1])
+
+        @pl.when(here[origin])
+        def _():
+            wait_recv(name, key, whole)
+            if origin[1] == 0:
+                buf = slab(name, key)
+                first = (rows if key[0] == "C" else 0) + origin[0] * rows
+                for comp in range(whole.shape[0]):
+                    for n in range(REACH):
+                        whole[comp, first + n] = whole[comp, first + n] + buf[comp, n]
+                return
+            for comp, row, col, at, width in landed(name, key):
+                span = slice(col, col + width)
+                whole[comp, row, span] = whole[comp, row, span] + recv_buf[at : at + width]
+
+    def take_sums(name, kind, whole, sent):
+        order = ORDERS[kind]
+        slabs = [key for key in keys_of(kind) if key[1][1] == 0]
+        wait_sends(name, slabs, whole)
+        if kind == "crossed":
+            for key, late in zip(slabs, ("A late", "C late")):
+                take_sum(name, key, whole)
+                send_done(name, order, whole, late)
+        else:
+            for key in order["C"] + order["A"]:
+                take_sum(name, key, whole)
+        for other in sent:
+            wait_sends(*other)
+        if name == ("f", 0):
+            take_state("v", STATE, v_ref, wide_v)
+        for key in order["B"] + order["E"]:
+            take_sum(name, key, whole)
+        if kind == "crossed":
+            for key in order["A late"]:
+                take_sum(name, key, whole)
+
+    def take_late(name, whole):
+        for key in CROSSED["C late"]:
+            take_sum(name, key, whole)
 
     loads[0].wait()
     pack("u", STATE, u_ref, 0)
@@ -359,15 +396,40 @@
         moved = pltpu.roll(values, (-c) % nz, axis=1)
         return jnp.where((lane + c >= 0) & (lane + c < nz), moved, 0.0)
 
-    def shift_motion():
-        for r in range(wide_rows):
-            for comp in range(3):
-                values = wide_u[comp, r]
-                for c in range(-NEAR, NEAR + 1):
-                    moved = shifted(values, c)
-                    if comp == 2 and c != 0:
-                        moved = moved + float(c)
-                    u_shift[c + NEAR, comp, r] = moved
+    def shifts(r):
+        return (0,) if r == wide_rows - 1 else range(-NEAR, NEAR + 1)
+
+    def shift_motion(r):
+        for comp in range(3):
+            values = wide_u[comp, r]
+            for c in shifts(r):
+                moved = shifted(values, c)
+                if comp == 2 and c != 0:
+                    moved = moved + float(c)
+                u_shift[c + NEAR, comp, r] = moved
+
+    def advance(step, r):
+        for comp in range(3):
+            speed = wide_v[comp, r] + force[step, comp, r] * inertia[r]
+            wide_v[comp, r] = speed
+            wide_u[comp, r] = wide_u[comp, r] + TIME_STEP * speed
+        shift_motion(r)
+
+    def shift_pressure(step, r):
+        values = strain[step, 0, r] * a_coef[r]
+        for c in shifts(r):
+            a_shift[c + NEAR, r] = shifted(values, c)
+
+    def just_in_time(make):
+        made = set()
+
+        def need(i, groups):
+            for r in sorted({i} | {i + a for a, _ in groups}):
+                if r not in made:
+                    made.add(r)
+                    make(r)
+
+        return need
 
     def materials():
         for r in range(wide_rows):
@@ -383,7 +445,7 @@
             inertia[r] = TIME_STEP / dens
             a_coef[r] = (9.0 / (VOLUME * VOLUME)) * (bulk - (5.0 / 3.0) * shear)
             stiff = (15.0 / VOLUME) * shear
-            for c in range(-NEAR, NEAR + 1):
+            for c in shifts(r):
                 b_shift[c + NEAR, r] = shifted(stiff, c)
 
     depth = lax.broadcasted_iota(jnp.int32, (cols, nz), 1)
@@ -421,7 +483,10 @@
     def back(values, c):
         return values if c == 0 else pltpu.roll(values, c % nz, axis=1)
 
-    def send_done(name, chunk, keys, whole):
+    def packed_of(name, kind, whole):
+        return [(name, [key for key in keys_of(kind) if key[1][1] != 0], whole)]
+
+    def send_done(name, keys, whole, chunk):
         pack(name, keys[chunk], whole, REACH)
         start_all(name, keys[chunk], whole)
 
@@ -450,11 +515,13 @@
                 by_stretch[k, i] = scale * (both_b * (by_stretch[k, i] * (1.0 / RADII[k])))
                 by_inverse[k, i] = scale
 
-    def strain_pass(send):
-        strain[...] = jnp.zeros(strain.shape, F32)
+    def strain_pass(sums_ref, need, send, far_rows):
         mid = pl.ds(REACH, cols)
-        for chunk, work in bond_order(rows):
+        for chunk, work in bond_order(rows, "ABCE"):
+            if chunk == "C":
+                far_rows()
             for i, groups in work:
+                need(i, groups)
                 own = own_motion(i)
                 sums = []
                 for a, b in groups:
@@ -468,113 +535,154 @@
                         sums.append(term)
                         returned.append(back(term, c))
                     at = pl.ds(REACH + b, cols)
-                    strain[0, i + a, at] = strain[0, i + a, at] + tree_sum(returned)
+                    sums_ref[0, i + a, at] = sums_ref[0, i + a, at] + tree_sum(returned)
                     sums = [tree_sum(sums)]
-                strain[0, i, mid] = strain[0, i, mid] + sums[0]
+                sums_ref[0, i, mid] = sums_ref[0, i, mid] + sums[0]
             send(chunk)
 
-    def force_pass(send):
-        force[...] = jnp.zeros(force.shape, F32)
+    def tensions_of(i, a, b, own_a):
+        found = []
+        for k, c in GROUPS[a, b]:
+            both_a = own_a + partner(a_shift, i, a, b, c, own_a)
+            found.append((c, by_inverse[k, i] * both_a + by_stretch[k, i]))
+        return found
+
+    def pull_origin(i, a, b, tensions, own):
+        at = pl.ds(REACH + b, cols)
+        base = (own[0][a], own[1][b], own[2])
+        total = tree_sum([tension for _, tension in tensions])
+        return [
+            tree_sum([t * u_shift[c + NEAR, comp, i + a, at] for c, t in tensions])
+            - base[comp] * total
+            for comp in range(3)
+        ]
+
+    def pull_partner(i, a, b, tensions, sums_ref):
         mid = pl.ds(REACH, cols)
-        for chunk, work in bond_order(rows):
+        at = pl.ds(REACH + b, cols)
+        pulled = [(c, back(tension, c)) for c, tension in tensions]
+        total = tree_sum([tension for _, tension in pulled])
+        for comp, shift in enumerate((float(a), float(b), 0.0)):
+            origin = tree_sum([t * u_shift[NEAR - c, comp, i, mid] for c, t in pulled])
+            end = u_shift[NEAR, comp, i + a, at] + shift
+            sums_ref[comp, i + a, at] = sums_ref[comp, i + a, at] + (origin - end * total)
+
+    def pull_both(i, a, b, tensions, own, sums_ref, sums):
+        at = pl.ds(REACH + b, cols)
+        returned = [[], [], []]
+        for c, tension in tensions:
+            y = bond_vector(i, a, b, c, own)
+            for comp in range(3):
+                term = tension * y[comp]
+                sums[comp].append(term)
+                returned[comp].append(back(term, c))
+        for comp in range(3):
+            sums_ref[comp, i + a, at] = sums_ref[comp, i + a, at] - tree_sum(returned[comp])
+
+    def force_pass(sums_ref, need, send):
+        mid = pl.ds(REACH, cols)
+        for chunk, work in bond_order(rows, "CABE"):
             for i, groups in work:
+                need(i, groups)
                 own = own_motion(i)
                 own_a = a_shift[NEAR, i, mid]
                 sums = [[], [], []]
                 for a, b in groups:
-                    at = pl.ds(REACH + b, cols)
-                    tensions = []
-                    for k, c in GROUPS[a, b]:
-                        both_a = own_a + partner(a_shift, i, a, b, c, own_a)
-                        tensions.append((c, by_inverse[k, i] * both_a + by_stretch[k, i]))
+                    tensions = tensions_of(i, a, b, own_a)
                     if (a, b) in AT_PARTNER:
-                        base = (own[0][a], own[1][b], own[2])
-                        shift = (float(a), float(b), 0.0)
-                        pulled = [(c, back(tension, c)) for c, tension in tensions]
-                        here_all = tree_sum([tension for _, tension in tensions])
-                        there_all = tree_sum([tension for _, tension in pulled])
-                        for comp in range(3):
-                            direct = tree_sum(
-                                [t * u_shift[c + NEAR, comp, i + a, at] for c, t in tensions]
-                            )
-                            sums[comp].append(direct - base[comp] * here_all)
-                            origin = tree_sum(
-                                [t * u_shift[NEAR - c, comp, i, mid] for c, t in pulled]
-                            )
-                            end = u_shift[NEAR, comp, i + a, at] + shift[comp]
-                            force[comp, i + a, at] = force[comp, i + a, at] + (
-                                origin - end * there_all
-                            )
+                        for comp, part in enumerate(pull_origin(i, a, b, tensions, own)):
+                            sums[comp].append(part)
+                        pull_partner(i, a, b, tensions, sums_ref)
                     else:
-                        returned = [[], [], []]
-                        for c, tension in tensions:
-                            y = bond_vector(i, a, b, c, own)
-                            for comp in range(3):
-                                term = tension * y[comp]
-                                sums[comp].append(term)
-                                returned[comp].append(back(term, c))
-                        for comp in range(3):
-                            force[comp, i + a, at] = force[comp, i + a, at] - tree_sum(
-                                returned[comp]
-                            )
+                        pull_both(i, a, b, tensions, own, sums_ref, sums)
                     sums = [[tree_sum(sums[comp])] for comp in range(3)]
                 for comp in range(3):
-                    force[comp, i, mid] = force[comp, i, mid] + sums[comp][0]
+                    sums_ref[comp, i, mid] = sums_ref[comp, i, mid] + sums[comp][0]
             send(chunk)
+
+    def last_force_pass(sums_ref, need, send):
+        mid = pl.ds(REACH, cols)
+        for chunk, work in bond_order(rows, "CABE"):
+            for i, groups in work:
+                leaving = [(a, b) for a, b in groups if b != 0 or i + a >= rows]
+                need(i, groups)
+                own_a = a_shift[NEAR, i, mid]
+                for a, b in leaving:
+                    tensions = tensions_of(i, a, b, own_a)
+                    for (k, _), (_, tension) in zip(GROUPS[a, b], tensions):
+                        by_stretch[k, i] = tension
+                    pull_partner(i, a, b, tensions, sums_ref)
+            send(chunk)
+        for i in range(rows):
+            own = own_motion(i)
+            own_a = a_shift[NEAR, i, mid]
+            sums = [[], [], []]
+            for a, b in GROUPS:
+                if b != 0 or i + a >= rows:
+                    tensions = [(c, by_stretch[k, i]) for k, c in GROUPS[a, b]]
+                    for comp, part in enumerate(pull_origin(i, a, b, tensions, own)):
+                        sums[comp].append(part)
+                else:
+                    tensions = tensions_of(i, a, b, own_a)
+                    pull_both(i, a, b, tensions, own, sums_ref, sums)
+                sums = [[tree_sum(sums[comp])] for comp in range(3)]
+            for comp in range(3):
+                sums_ref[comp, i, mid] = sums_ref[comp, i, mid] + sums[comp][0]
 
     for load in loads[3:]:
         load.wait()
     weights()
-    take_state("u", u_ref, wide_u)
+    strain[...] = jnp.zeros(strain.shape, F32)
+    force[...] = jnp.zeros(force.shape, F32)
+    take_state("u", [key for key in STATE if key[1][0] == 0], u_ref, wide_u)
     start_all("m", STATE, mat_f32)
-    shift_motion()
-
+
+    sent = [("u", STATE, u_ref)]
     for step in range(STEPS):
         last = step == STEPS - 1
         name = ("t", step)
-        every = keys_of("sum")
-        strain_pass(lambda chunk, name=name: send_done(name, chunk, CHUNKS, strain))
+        whole = strain.at[step]
+        if step == 0:
+            make = shift_motion
+            far = [key for key in STATE if key[1][0] != 0]
+            far_rows = functools.partial(take_state, "u", far, u_ref, wide_u)
+        else:
+            make = functools.partial(advance, step - 1)
+            far_rows = functools.partial(take_late, ("f", step - 1), force.at[step - 1])
+        strain_pass(
+            whole, just_in_time(make), functools.partial(send_done, name, CHUNKS, whole), far_rows
+        )
         if step == 0:
             start_all("v", STATE, v_ref)
-            take_state("m", mat_f32, wide_m)
+            take_state("m", STATE, mat_f32, wide_m)
             materials()
         prepare()
-        take_sums(name, every, strain)
-
-        for r in range(wide_rows):
-            values = strain[0, r] * a_coef[r]
-            for c in range(-NEAR, NEAR + 1):
-                a_shift[c + NEAR, r] = shifted(values, c)
-
-        wait_sends(name, [key for key in every if key[1][1] != 0], strain)
+        take_sums(name, "sum", whole, sent)
+        sent = packed_of(name, "sum", whole)
+        if step == 0:
+            sent = sent + [("m", STATE, mat_f32), ("v", STATE, v_ref)]
+
         name = ("f", step)
-        keys = FINAL if last else CHUNKS
-        every = keys_of("final" if last else "sum")
-        force_pass(lambda chunk, name=name, keys=keys: send_done(name, chunk, keys, force))
-        if step == 0:
-            take_state("v", v_ref, wide_v)
-        take_sums(name, every, force)
-        if not last:
-            for r in range(wide_rows):
-                for comp in range(3):
-                    speed = wide_v[comp, r] + force[comp, r] * inertia[r]
-                    wide_v[comp, r] = speed
-                    wide_u[comp, r] = wide_u[comp, r] + TIME_STEP * speed
-
-            shift_motion()
-        else:
+        whole = force.at[step]
+        kind = "final" if last else "crossed"
+        run = last_force_pass if last else force_pass
+        run(
+            whole,
+            just_in_time(functools.partial(shift_pressure, step)),
+            functools.partial(send_done, name, ORDERS[kind], whole),
+        )
+        packed_now = packed_of(name, kind, whole)
+        take_sums(name, kind, whole, sent + packed_now if last else sent)
+        sent = packed_now
+        if last:
             mid = pl.ds(REACH, cols)
             for r in range(rows):
                 for comp in range(3):
-                    pull = force[comp, r, mid]
+                    pull = force[step, comp, r, mid]
                     speed = wide_v[comp, r, mid] + pull * inertia[r, mid]
                     out_f[comp, r] = pull
                     out_v[comp, r] = speed
                     out_u[comp, r] = wide_u[comp, r, mid] + TIME_STEP * speed
-
-        wait_sends(name, [key for key in every if key[1][1] != 0], force)
-    for name, own in (("u", u_ref), ("m", mat_f32), ("v", v_ref)):
-        wait_sends(name, STATE, own)
 
 
 def hand_over(u_in, v_in, f_in, u_out, v_out, f_out):
@@ -621,8 +729,8 @@
             buffer(5, wide_rows, padded),
             buffer(wide_rows, padded),
             buffer(wide_rows, padded),
-            buffer(1, wide_rows, padded),
-            buffer(3, wide_rows, padded),
+            buffer(STEPS, 1, wide_rows, padded),
+            buffer(STEPS, 3, wide_rows, padded),
             buffer(packed),
             buffer(packed),
             buffer(3, REACH, cols),
@@ -631,8 +739,8 @@
             buffer(STEPS, 2, 1, REACH, padded),
             buffer(STEPS, 2, 3, REACH, padded),
             pltpu.SemaphoreType.DMA((7,)),
-            pltpu.SemaphoreType.DMA((len(stages()), 12)),
-            pltpu.SemaphoreType.DMA((len(stages()), 12)),
+            pltpu.SemaphoreType.DMA((len(stages()), SLOTS)),
+            pltpu.SemaphoreType.DMA((len(stages()), SLOTS)),
         ],
         compiler_params=pltpu.CompilerParams(
             collective_id=0, has_side_effects=True, vmem_limit_bytes=67_043_328

time: 34.8 us -> 34.1 us (0.980)
  Pallas kernels: 34 us -> 33.3 us
    pallas_call x1, Pallas kernels: 32.3 us -> 31.6 us  [on_device(): pl.pallas_call(functools.partial(kernel, lax.axis_size('gx'), lax.axis_si...]
where the time goes in v3:
time: 34.1 us; the launch traced here: 33.9 us
  Pallas kernels  33.3 us (98%)
  between operations  0.64 us (2%)
    pallas_call x1, Pallas kernels, on_device(): pl.pallas_call(functools.partial(kernel, lax.axis_size('gx'), lax.axis_si...  31.6 us
    pallas_call x1, Pallas kernels, on_device(): pl.pallas_call(hand_over, out_shape=(own, own, own), in_specs=[vmem] * 3,...  1.7 us

profile of v3, /device:TPU:0, one launch (start us, length us, event | category | flops | bytes accessed | tf_op | source)
XLA Modules:
  0.0 33.9 jit_solution(10575305584738527277)
XLA Ops:
  0.6 31.6 %peridynamics.1 = (f32[3,8,8,128]{3,2,1,0:T(8,128)}, f32[3,8,8,128]{3,2,1,0:T(8,128)}, f32[3,8,8,128]{3,2,1,0:T(8,128)}) custom-call(f32[3,8,8,128]{3,2,1,0:T(8,128)} %u_hbm.1, f32[3,8,8,128]{3,2,1,0:T(8,128)} %v_hbm.1, s32[61,8,8,128]{3,2,1,0:T(8,128)} %intact_hbm.1, s32[8,8,128]{2,1,0:T(8,128)} %mat_hbm.1, f32[8]{0:T(128)} %bulk_hbm.1, f32[8]{0:T(128)} %shear_hbm.1, ...), custom_call_target="tpu_custom_call" | custom-call | tf_op jit(solution)/shard_map/peridynamics/pallas_call | solution.py:707
  32.2 1.7 %hand_over.1 = (f32[3,8,8,128]{3,2,1,0:T(8,128)}, f32[3,8,8,128]{3,2,1,0:T(8,128)}, f32[3,8,8,128]{3,2,1,0:T(8,128)}) custom-call(f32[3,8,8,128]{3,2,1,0:T(8,128)} %get-tuple-element.6.u_in, f32[3,8,8,128]{3,2,1,0:T(8,128)} %get-tuple-element.7.v_in, f32[3,8,8,128]{3,2,1,0:T(8,128)} %get-tuple-element.8.f_in), custom_call_target="tpu_custom_call" | custom-call | tf_op jit(solution)/shard_map/hand_over/pallas_call | solution.py:750

commit v4 on v3

--- a/solution.py
+++ b/solution.py
@@ -359,16 +359,16 @@
             take_state("v", STATE, v_ref, wide_v)
         for key in order["B"] + order["E"]:
             take_sum(name, key, whole)
-        if kind == "crossed":
-            for key in order["A late"]:
-                take_sum(name, key, whole)
-
-    def take_late(name, whole):
-        for key in CROSSED["C late"]:
+
+    def take_late(name, whole, chunk):
+        for key in CROSSED[chunk + " late"]:
             take_sum(name, key, whole)
 
     loads[0].wait()
     pack("u", STATE, u_ref, 0)
+    loads[2].wait()
+    mat_f32[0] = mat_ref[...].astype(F32)
+    pack("m", STATE, mat_f32, 0)
 
     on_x = (gx > 0).astype(jnp.int32) + (gx < grid_rows - 1).astype(jnp.int32)
     on_y = (gy > 0).astype(jnp.int32) + (gy < grid_cols - 1).astype(jnp.int32)
@@ -376,9 +376,6 @@
     start_all("u", STATE, u_ref)
 
     loads[1].wait()
-    loads[2].wait()
-    mat_f32[0] = mat_ref[...].astype(F32)
-    pack("m", STATE, mat_f32, 0)
     pack("v", STATE, v_ref, 0)
 
     wide_u[...] = jnp.zeros(wide_u.shape, F32)
@@ -515,11 +512,13 @@
                 by_stretch[k, i] = scale * (both_b * (by_stretch[k, i] * (1.0 / RADII[k])))
                 by_inverse[k, i] = scale
 
-    def strain_pass(sums_ref, need, send, far_rows):
+    def stays(i, a, b):
+        return b == 0 and i + a < rows
+
+    def strain_pass(sums_ref, order, need, arrive, send):
         mid = pl.ds(REACH, cols)
-        for chunk, work in bond_order(rows, "ABCE"):
-            if chunk == "C":
-                far_rows()
+        for chunk, work in order:
+            arrive(chunk)
             for i, groups in work:
                 need(i, groups)
                 own = own_motion(i)
@@ -634,8 +633,22 @@
     weights()
     strain[...] = jnp.zeros(strain.shape, F32)
     force[...] = jnp.zeros(force.shape, F32)
+    start_all("m", STATE, mat_f32)
+
+    def near(i, groups):
+        return [(a, b) for a, b in groups if stays(i, a, b)]
+
+    def rest(i, groups):
+        return [(a, b) for a, b in groups if not stays(i, a, b)]
+
+    strain_pass(
+        strain.at[0],
+        [("", [(i, near(i, GROUPS)) for i in range(rows)])],
+        just_in_time(shift_motion),
+        lambda chunk: None,
+        lambda chunk: None,
+    )
     take_state("u", [key for key in STATE if key[1][0] == 0], u_ref, wide_u)
-    start_all("m", STATE, mat_f32)
 
     sent = [("u", STATE, u_ref)]
     for step in range(STEPS):
@@ -644,14 +657,28 @@
         whole = strain.at[step]
         if step == 0:
             make = shift_motion
-            far = [key for key in STATE if key[1][0] != 0]
-            far_rows = functools.partial(take_state, "u", far, u_ref, wide_u)
+            order = [
+                (chunk, [(i, rest(i, groups)) for i, groups in work])
+                for chunk, work in bond_order(rows, "ABCE")
+            ]
         else:
             make = functools.partial(advance, step - 1)
-            far_rows = functools.partial(take_late, ("f", step - 1), force.at[step - 1])
-        strain_pass(
-            whole, just_in_time(make), functools.partial(send_done, name, CHUNKS, whole), far_rows
-        )
+            order = bond_order(rows, "BACE")
+
+        def arrive(chunk, step=step):
+            if step == 0:
+                if chunk == "C":
+                    far = [key for key in STATE if key[1][0] != 0]
+                    take_state("u", far, u_ref, wide_u)
+            elif chunk in ("A", "C"):
+                take_late(("f", step - 1), force.at[step - 1], chunk)
+
+        def send(chunk, step=step, name=name, whole=whole):
+            ready = {"B": [], "A": ["A", "B"]} if step else {}
+            for done in ready.get(chunk, [chunk]):
+                send_done(name, CHUNKS, whole, done)
+
+        strain_pass(whole, order, just_in_time(make), arrive, send)
         if step == 0:
             start_all("v", STATE, v_ref)
             take_state("m", STATE, mat_f32, wide_m)

time: 34.1 us -> 32.9 us (0.965)
  Pallas kernels: 33.3 us -> 32.1 us
    pallas_call x1, Pallas kernels: 31.6 us -> 30.4 us  [on_device(): pl.pallas_call(functools.partial(kernel, lax.axis_size('gx'), lax.axis_si...]
where the time goes in v4:
time: 32.9 us; the launch traced here: 32.7 us
  Pallas kernels  32.1 us (98%)
  between operations  0.64 us (2%)
    pallas_call x1, Pallas kernels, on_device(): pl.pallas_call(functools.partial(kernel, lax.axis_size('gx'), lax.axis_si...  30.4 us
    pallas_call x1, Pallas kernels, on_device(): pl.pallas_call(hand_over, out_shape=(own, own, own), in_specs=[vmem] * 3,...  1.7 us

profile of v4, /device:TPU:0, one launch (start us, length us, event | category | flops | bytes accessed | tf_op | source)
XLA Modules:
  0.0 32.7 jit_solution(4963496042020800864)
XLA Ops:
  0.6 30.4 %peridynamics.1 = (f32[3,8,8,128]{3,2,1,0:T(8,128)}, f32[3,8,8,128]{3,2,1,0:T(8,128)}, f32[3,8,8,128]{3,2,1,0:T(8,128)}) custom-call(f32[3,8,8,128]{3,2,1,0:T(8,128)} %u_hbm.1, f32[3,8,8,128]{3,2,1,0:T(8,128)} %v_hbm.1, s32[61,8,8,128]{3,2,1,0:T(8,128)} %intact_hbm.1, s32[8,8,128]{2,1,0:T(8,128)} %mat_hbm.1, f32[8]{0:T(128)} %bulk_hbm.1, f32[8]{0:T(128)} %shear_hbm.1, ...), custom_call_target="tpu_custom_call" | custom-call | tf_op jit(solution)/shard_map/peridynamics/pallas_call | solution.py:734
  31.0 1.7 %hand_over.1 = (f32[3,8,8,128]{3,2,1,0:T(8,128)}, f32[3,8,8,128]{3,2,1,0:T(8,128)}, f32[3,8,8,128]{3,2,1,0:T(8,128)}) custom-call(f32[3,8,8,128]{3,2,1,0:T(8,128)} %get-tuple-element.6.u_in, f32[3,8,8,128]{3,2,1,0:T(8,128)} %get-tuple-element.7.v_in, f32[3,8,8,128]{3,2,1,0:T(8,128)} %get-tuple-element.8.f_in), custom_call_target="tpu_custom_call" | custom-call | tf_op jit(solution)/shard_map/hand_over/pallas_call | solution.py:777

commit v5 on v4

--- a/solution.py
+++ b/solution.py
@@ -86,9 +86,11 @@
     own = {(r, c) for r in range(rows) for c in range(cols)}
     wide = own | {(r + a, c + b) for r, c in own for a, b in GROUPS}
     sender = own if kind == "state" else wide
-    if kind == "crossed":
+    if kind == "crossed" and dx == 0:
         sender = {(r + x, c) for r, c in wide for x in (-rows, 0, rows)}
     receiver = own if kind == "final" else wide
+    if kind == "crossed" and dx != 0:
+        receiver = {(r, c + y) for r, c in wide for y in (-cols, 0, cols)}
     first, end = {
         "A": (0, REACH),
         "B": (REACH, rows - REACH),
@@ -122,8 +124,6 @@
     place, at = {}, 0
     for number, (_, kind, comps) in enumerate(stages()):
         for key in keys_of(kind):
-            if key[1][1] == 0:
-                continue
             runs = spans(rows, cols, key, kind)
             size = round_up(comps * sum(width for _, _, width in runs), 8)
             place[number, key] = (at, size, runs)
@@ -176,11 +176,6 @@
     force,
     send_buf,
     recv_buf,
-    u_slab,
-    m_slab,
-    v_slab,
-    t_slab,
-    f_slab,
     local_sem,
     send_sem,
     recv_sem,
@@ -229,33 +224,12 @@
     for load in loads:
         load.start()
 
-    def side(value):
-        return 0 if value < 0 else 1
-
-    def slab(name, key):
-        if name == "u":
-            return u_slab
-        if name == "m":
-            return m_slab
-        if name == "v":
-            return v_slab
-        buf = t_slab if name[0] == "t" else f_slab
-        return buf.at[name[1], side(-key[1][0])]
-
-    def ends(name, key, whole):
-        number = number_of[name]
-        if key[1][1] == 0:
-            first = rows if key[0] == "C" else 0
-            return whole.at[:, first : first + REACH], slab(name, key)
-        at, size, _ = place[number, key]
-        return send_buf.at[at : at + size], recv_buf.at[at : at + size]
-
-    def copy_to(name, key, whole):
+    def copy_to(name, key):
         dx, dy = key[1]
-        source, target = ends(name, key, whole)
+        at, size, _ = place[number_of[name], key]
         return pltpu.make_async_remote_copy(
-            src_ref=source,
-            dst_ref=target,
+            src_ref=send_buf.at[at : at + size],
+            dst_ref=recv_buf.at[at : at + size],
             send_sem=send_sem.at[number_of[name], SLOT[key]],
             recv_sem=recv_sem.at[number_of[name], SLOT[key]],
             device_id=(gx + dx, gy + dy),
@@ -266,8 +240,6 @@
         number = number_of[name]
         comps = listed[number][2]
         for key in keys:
-            if key[1][1] == 0:
-                continue
             at, _, runs = place[number, key]
             for comp in range(comps):
                 for row, col, width in runs:
@@ -275,15 +247,16 @@
                     send_buf[at : at + width] = whole[comp, row, begin : begin + width]
                     at += width
 
-    def start_all(name, keys, whole):
+    def start_all(name, keys):
         for key in keys:
 
             @pl.when(here[key[1]])
             def _(key=key):
-                copy_to(name, key, whole).start()
-
-    def wait_recv(name, key, whole):
-        _, target = ends(name, key, whole)
+                copy_to(name, key).start()
+
+    def wait_recv(name, key):
+        at, size, _ = place[number_of[name], key]
+        target = recv_buf.at[at : at + size]
         pltpu.make_async_remote_copy(
             src_ref=target,
             dst_ref=target,
@@ -293,12 +266,12 @@
             device_id_type=MESH,
         ).wait_recv()
 
-    def wait_sends(name, keys, whole):
+    def wait_sends(name, keys):
         for key in keys:
 
             @pl.when(here[key[1]])
             def _(key=key):
-                copy_to(name, key, whole).wait_send()
+                copy_to(name, key).wait_send()
 
     def landed(name, key):
         number = number_of[name]
@@ -309,19 +282,13 @@
                 yield comp, row - dx * rows, REACH + col - dy * cols, at, width
                 at += width
 
-    def take_state(name, keys, own, wide):
+    def take_state(name, keys, wide):
         for key in keys:
             origin = (-key[1][0], -key[1][1])
 
             @pl.when(here[origin])
-            def _(key=key, origin=origin):
-                wait_recv(name, key, own)
-                if origin[1] == 0:
-                    buf = slab(name, key)
-                    for comp in range(own.shape[0]):
-                        for r in range(REACH):
-                            wide[comp, rows + r, REACH : REACH + cols] = buf[comp, r]
-                    return
+            def _(key=key):
+                wait_recv(name, key)
                 for comp, row, col, at, width in landed(name, key):
                     wide[comp, row, col : col + width] = recv_buf[at : at + width]
 
@@ -330,24 +297,15 @@
 
         @pl.when(here[origin])
         def _():
-            wait_recv(name, key, whole)
-            if origin[1] == 0:
-                buf = slab(name, key)
-                first = (rows if key[0] == "C" else 0) + origin[0] * rows
-                for comp in range(whole.shape[0]):
-                    for n in range(REACH):
-                        whole[comp, first + n] = whole[comp, first + n] + buf[comp, n]
-                return
+            wait_recv(name, key)
             for comp, row, col, at, width in landed(name, key):
                 span = slice(col, col + width)
                 whole[comp, row, span] = whole[comp, row, span] + recv_buf[at : at + width]
 
     def take_sums(name, kind, whole, sent):
         order = ORDERS[kind]
-        slabs = [key for key in keys_of(kind) if key[1][1] == 0]
-        wait_sends(name, slabs, whole)
         if kind == "crossed":
-            for key, late in zip(slabs, ("A late", "C late")):
+            for key, late in ((order["C"][0], "A late"), (order["A"][0], "C late")):
                 take_sum(name, key, whole)
                 send_done(name, order, whole, late)
         else:
@@ -356,7 +314,7 @@
         for other in sent:
             wait_sends(*other)
         if name == ("f", 0):
-            take_state("v", STATE, v_ref, wide_v)
+            take_state("v", STATE, wide_v)
         for key in order["B"] + order["E"]:
             take_sum(name, key, whole)
 
@@ -373,7 +331,7 @@
     on_x = (gx > 0).astype(jnp.int32) + (gx < grid_rows - 1).astype(jnp.int32)
     on_y = (gy > 0).astype(jnp.int32) + (gy < grid_cols - 1).astype(jnp.int32)
     pl.semaphore_wait(barrier, (1 + on_x) * (1 + on_y) - 1)
-    start_all("u", STATE, u_ref)
+    start_all("u", STATE)
 
     loads[1].wait()
     pack("v", STATE, v_ref, 0)
@@ -480,12 +438,9 @@
     def back(values, c):
         return values if c == 0 else pltpu.roll(values, c % nz, axis=1)
 
-    def packed_of(name, kind, whole):
-        return [(name, [key for key in keys_of(kind) if key[1][1] != 0], whole)]
-
     def send_done(name, keys, whole, chunk):
         pack(name, keys[chunk], whole, REACH)
-        start_all(name, keys[chunk], whole)
+        start_all(name, keys[chunk])
 
     def weights():
         @pl.loop(0, rows)
@@ -633,7 +588,7 @@
     weights()
     strain[...] = jnp.zeros(strain.shape, F32)
     force[...] = jnp.zeros(force.shape, F32)
-    start_all("m", STATE, mat_f32)
+    start_all("m", STATE)
 
     def near(i, groups):
         return [(a, b) for a, b in groups if stays(i, a, b)]
@@ -648,9 +603,9 @@
         lambda chunk: None,
         lambda chunk: None,
     )
-    take_state("u", [key for key in STATE if key[1][0] == 0], u_ref, wide_u)
-
-    sent = [("u", STATE, u_ref)]
+    take_state("u", [key for key in STATE if key[1][0] == 0], wide_u)
+
+    sent = [("u", STATE)]
     for step in range(STEPS):
         last = step == STEPS - 1
         name = ("t", step)
@@ -669,7 +624,7 @@
             if step == 0:
                 if chunk == "C":
                     far = [key for key in STATE if key[1][0] != 0]
-                    take_state("u", far, u_ref, wide_u)
+                    take_state("u", far, wide_u)
             elif chunk in ("A", "C"):
                 take_late(("f", step - 1), force.at[step - 1], chunk)
 
@@ -680,14 +635,14 @@
 
         strain_pass(whole, order, just_in_time(make), arrive, send)
         if step == 0:
-            start_all("v", STATE, v_ref)
-            take_state("m", STATE, mat_f32, wide_m)
+            start_all("v", STATE)
+            take_state("m", STATE, wide_m)
             materials()
         prepare()
         take_sums(name, "sum", whole, sent)
-        sent = packed_of(name, "sum", whole)
+        sent = [(name, keys_of("sum"))]
         if step == 0:
-            sent = sent + [("m", STATE, mat_f32), ("v", STATE, v_ref)]
+            sent = sent + [("m", STATE), ("v", STATE)]
 
         name = ("f", step)
         whole = force.at[step]
@@ -698,7 +653,7 @@
             just_in_time(functools.partial(shift_pressure, step)),
             functools.partial(send_done, name, ORDERS[kind], whole),
         )
-        packed_now = packed_of(name, kind, whole)
+        packed_now = [(name, keys_of(kind))]
         take_sums(name, kind, whole, sent + packed_now if last else sent)
         sent = packed_now
         if last:
@@ -760,11 +715,6 @@
             buffer(STEPS, 3, wide_rows, padded),
             buffer(packed),
             buffer(packed),
-            buffer(3, REACH, cols),
-            buffer(1, REACH, cols),
-            buffer(3, REACH, cols),
-            buffer(STEPS, 2, 1, REACH, padded),
-            buffer(STEPS, 2, 3, REACH, padded),
             pltpu.SemaphoreType.DMA((7,)),
             pltpu.SemaphoreType.DMA((len(stages()), SLOTS)),
             pltpu.SemaphoreType.DMA((len(stages()), SLOTS)),

time: 32.9 us -> 32.8 us (level)
  no operation moved by 1% of the time
where the time goes in v5:
time: 32.8 us; the launch traced here: 32.6 us
  Pallas kernels  32 us (98%)
  between operations  0.64 us (2%)
    pallas_call x1, Pallas kernels, on_device(): pl.pallas_call(functools.partial(kernel, lax.axis_size('gx'), lax.axis_si...  30.3 us
    pallas_call x1, Pallas kernels, on_device(): pl.pallas_call(hand_over, out_shape=(own, own, own), in_specs=[vmem] * 3,...  1.7 us

profile of v5, /device:TPU:0, one launch (start us, length us, event | category | flops | bytes accessed | tf_op | source)
XLA Modules:
  0.0 32.6 jit_solution(5055070141257522355)
XLA Ops:
  0.6 30.3 %peridynamics.1 = (f32[3,8,8,128]{3,2,1,0:T(8,128)}, f32[3,8,8,128]{3,2,1,0:T(8,128)}, f32[3,8,8,128]{3,2,1,0:T(8,128)}) custom-call(f32[3,8,8,128]{3,2,1,0:T(8,128)} %u_hbm.1, f32[3,8,8,128]{3,2,1,0:T(8,128)} %v_hbm.1, s32[61,8,8,128]{3,2,1,0:T(8,128)} %intact_hbm.1, s32[8,8,128]{2,1,0:T(8,128)} %mat_hbm.1, f32[8]{0:T(128)} %bulk_hbm.1, f32[8]{0:T(128)} %shear_hbm.1, ...), custom_call_target="tpu_custom_call" | custom-call | tf_op jit(solution)/shard_map/peridynamics/pallas_call | solution.py:689
  30.9 1.7 %hand_over.1 = (f32[3,8,8,128]{3,2,1,0:T(8,128)}, f32[3,8,8,128]{3,2,1,0:T(8,128)}, f32[3,8,8,128]{3,2,1,0:T(8,128)}) custom-call(f32[3,8,8,128]{3,2,1,0:T(8,128)} %get-tuple-element.6.u_in, f32[3,8,8,128]{3,2,1,0:T(8,128)} %get-tuple-element.7.v_in, f32[3,8,8,128]{3,2,1,0:T(8,128)} %get-tuple-element.8.f_in), custom_call_target="tpu_custom_call" | custom-call | tf_op jit(solution)/shard_map/hand_over/pallas_call | solution.py:727
